TPU v7x, 128 devices: a whole 4x4x4 slice. The times are simulated.
128 devices in a mesh: shot: 8 (over z, core), bin: 16 (over y, x).
Axes of the slice: x: 4, y: 4, z: 4, core: 2. Of those that a mesh axis runs over, the one named last changes fastest.
Arguments:
- traces: bfloat16 [32768, 2048], P(('shot', 'bin')), may hold values from -6 to 6
- shot_filter: bfloat16 [128, 128], P(('shot', 'bin')), may hold values from -0.5 to 0.5
- channel_gain: float32 [256], replicated, may hold values from 0.5 to 2
- bin_owner: int32 [32768, 1], P(('shot', 'bin')), may hold values from 0 to 127; in each aligned block of 256 rows (0 to 255, 256 to 511, ...) at most 4 rows name the same one
- bin_slot: int32 [32768], P(('shot', 'bin')), may hold values from 0 to 15
- offset_class: int32 [32768], P(('shot', 'bin')), may hold values from 0 to 31
- dip_filter: bfloat16 [9, 31], replicated, may hold values from -0.375 to 0.375
- nmo_start: int32 [32, 2048], replicated, may hold values from 0 to 2040, as said below
- nmo_weights: bfloat16 [32, 8, 2048], replicated, may hold values from -2.09375 to 2.09375
Outputs:
- stacked: float32 [16, 128, 2048], P('shot', 'bin')
Inputs may be any that keep to these rules, and one draw needn't show every extreme that they name: `bin_owner`: among the rows of one device, at most 4 name any one block. `nmo_start`: band starts leave room for all 8 taps and lie at most 64 samples before their output sample.
All inputs are finite; a program needn't handle non-finite values.
Results may differ from a plain program's by a relative error of at most 0.0042.
Values may be sent and summed in bfloat16 or wider, within the bound.
No kernel may reach another device: no remote copies, remote signals or barrier semaphores. Data moves between devices by JAX's collectives and lax.ppermute only.
A program may use at most 256 MiB of HBM per device.

v0:
```python
import math

import jax
import jax.numpy as jnp
from jax import lax
from jax.experimental import pallas as pl
from jax.experimental.pallas import tpu as pltpu
from jax.sharding import PartitionSpec as P

LANES = 128
IL_DEV = 2
XL_DEV = 8
CAP = 4
HALVES = 2
F32 = jnp.float32
BF16 = jnp.bfloat16


def iota(shape, dim):
    return lax.broadcasted_iota(jnp.int32, shape, dim)


def send_kernel(traces, shot_filter, gain, owner, slot, offset, out, placed, filtered):
    rows, samples = traces.shape
    blocks = samples // LANES
    half = samples // HALVES
    offsets = 32
    slots = slot[...]
    hi = (slots % XL_DEV) * IL_DEV + slots // XL_DEV
    lo = offset[...]
    lane_row = iota((LANES, rows), 0)
    table = jnp.where(lane_row == 0, 1.0, 0.0)
    table = jnp.where(lane_row == 1, jnp.broadcast_to(hi.astype(F32), table.shape), table)
    table = jnp.where(lane_row == 2, jnp.broadcast_to(lo.astype(F32), table.shape), table)
    table = jnp.where(lane_row == 3, jnp.broadcast_to(gain[...], table.shape), table)
    table = jnp.where(lane_row == 4, jnp.broadcast_to(owner[...].astype(F32), table.shape), table)
    columns = table.T
    gain_column = columns[:, 3:4]
    owner_column = columns[:, 4:5].astype(jnp.int32)
    codes = jnp.where(iota(columns.shape, 1) < 3, columns, 0.0).astype(BF16)
    owner_row = owner[...]
    same = (owner_column == owner_row) & (iota((rows, rows), 0) < iota((rows, rows), 1))
    rank = jnp.sum(jnp.where(same, 1.0, 0.0), axis=0, keepdims=True).astype(jnp.int32)
    target = owner_row * (CAP * HALVES) + rank
    out_rows = out.shape[0]
    row_ids = iota((out_rows, rows), 0)
    for h in range(HALVES):
        placed[:, h * rows : (h + 1) * rows] = jnp.where(
            row_ids == target + h * CAP, 1.0, 0.0
        ).astype(BF16)
    taps = jnp.broadcast_to(shot_filter[...].astype(F32), (LANES, LANES))
    circulant = pltpu.roll(taps, 0, 1, stride=1, stride_axis=0)
    later = iota((LANES, LANES), 0) > iota((LANES, LANES), 1)
    before = jnp.where(later, circulant, 0.0).astype(BF16)
    centre = jnp.where(later, 0.0, circulant).astype(BF16)
    matrix = jnp.concatenate([before, centre], axis=0)
    for j in range(blocks):
        if j == 0:
            value = jnp.dot(traces[:, :LANES], centre, preferred_element_type=F32)
        else:
            value = jnp.dot(
                traces[:, (j - 1) * LANES : (j + 1) * LANES], matrix, preferred_element_type=F32
            )
        h, at = divmod(j * LANES, half)
        filtered[h * rows : (h + 1) * rows, at : at + LANES] = (value * gain_column).astype(BF16)
    for h in range(HALVES):
        filtered[h * rows : (h + 1) * rows, half:] = codes
    width = 2 * LANES
    for n in range(0, filtered.shape[1], width):
        stop = min(n + width, filtered.shape[1])
        out[:, n:stop] = jnp.dot(
            placed[...], filtered[:, n:stop], preferred_element_type=F32
        ).astype(BF16)


def stack_kernel(arrived, dip, start, weights, centre, right, left, windows, dips, dipped):
    slots = arrived.shape[0]
    half = arrived.shape[1] - LANES
    offsets, samples = start.shape
    blocks = samples // LANES
    lines = IL_DEV * offsets
    cells = XL_DEV * lines
    taps_x = dip.shape[0]
    rim = XL_DEV // 2
    out_lines = 2 * XL_DEV
    codes = arrived[:, half:]
    rows = codes.astype(F32).T
    code = jnp.where(rows[0:1] > 0.5, rows[1:2] * offsets + rows[2:3], -1.0).astype(jnp.int32)
    part = (iota((1, slots), 1) // CAP) % HALVES
    cell_ids = iota((cells, slots), 0)
    members = []
    for h in range(HALVES):
        hit = cell_ids == jnp.where(part == h, code, -1)
        members.append(jnp.where(hit, 1.0, 0.0).astype(BF16))
    fold = jnp.dot(members[0], codes, preferred_element_type=F32)[:, 0:1]
    scale = 1.0 / jnp.maximum(fold, 1.0)
    zero = jnp.zeros((lines, LANES), BF16)
    for x in range(XL_DEV):
        windows[0, :, 2 * x * LANES : (2 * x + 1) * LANES] = zero
        windows[blocks, :, (2 * x + 1) * LANES : (2 * x + 2) * LANES] = zero
    width = 2 * LANES
    for h in range(HALVES):
        for n in range(0, half, width):
            binned = (
                jnp.dot(members[h], arrived[:, n : n + width], preferred_element_type=F32) * scale
            ).astype(BF16)
            for b in range(width // LANES):
                block = (h * half + n) // LANES + b
                for x in range(XL_DEV):
                    piece = binned[x * lines : (x + 1) * lines, b * LANES : (b + 1) * LANES]
                    windows[block, :, (2 * x + 1) * LANES : (2 * x + 2) * LANES] = piece
                    windows[block + 1, :, 2 * x * LANES : (2 * x + 1) * LANES] = piece
    bands = []
    for a in range(taps_x):
        spread = jnp.broadcast_to(dip[a : a + 1, :], (2 * LANES, 2 * LANES))
        band = pltpu.roll(spread, 0, 1, stride=1, stride_axis=0)
        bands.append(band[:, :LANES].astype(BF16))
    none = jnp.zeros((2 * LANES, LANES), BF16)
    for d in range(taps_x + 1):
        dips[d * width : (d + 1) * width, :LANES] = bands[d] if d < taps_x else none
        dips[d * width : (d + 1) * width, LANES:] = bands[d - 1] if d > 0 else none

    group = dipped.shape[0] // 3

    def filter_group(g, carry):
        first = g * group
        for pair in range(out_lines // 2):
            low = max(0, 2 * pair - 2 * rim)
            high = min(XL_DEV, 2 * pair + 2)
            d = low - 2 * pair + 2 * rim
            lhs = windows[pl.ds(first, group), :, low * width : high * width]
            value = jnp.dot(
                lhs.reshape(group * lines, (high - low) * width),
                dips[d * width : (d + high - low) * width, :],
                preferred_element_type=F32,
            )
            for m in range(group):
                for i in range(IL_DEV):
                    for s in range(2):
                        line = (2 * pair + s - rim) % out_lines
                        at = m * lines + i * offsets
                        dipped[first + m, pl.ds(i * out_lines + line, offsets, stride=2 * out_lines), :] = (
                            value[at : at + offsets, s * LANES : (s + 1) * LANES]
                        )
        return carry

    lax.fori_loop(0, 3, filter_group, 0)

    tile = 8
    groups = 2 * LANES // tile
    span = 2 * out_lines
    sublane = iota((tile, LANES), 0)
    root = 1.0 / math.sqrt(offsets)

    def move_out(j, carry):
        at = pl.multiple_of(j * LANES, LANES)
        firsts = start[:, pl.ds(at, LANES)] + (LANES // 2 - at)
        total = jnp.zeros((span, LANES), F32)
        for o in range(offsets):
            first = jnp.broadcast_to(firsts[o : o + 1, :], (tile, LANES))
            turned = weights[o, :, pl.ds(at, LANES)].astype(F32)
            for bit in (1, 2, 4):
                turned = jnp.where(
                    (first & bit) != 0, pltpu.roll(turned, bit, 0), turned
                )
            place = (first - sublane + (tile - 1)) >> 3
            band = jnp.concatenate(
                [jnp.where(place == g, turned, 0.0) for g in range(groups)], axis=0
            ).astype(BF16)
            rows = pl.ds(o * span, span)
            lhs = jnp.concatenate(
                [dipped[j, rows, :].astype(BF16), dipped[j + 1, rows, :].astype(BF16)], axis=1
            )
            total = total + jnp.dot(lhs, band, preferred_element_type=F32)
        total = total * root
        for i in range(IL_DEV):
            base = i * out_lines
            centre[i, :, pl.ds(at, LANES)] = total[base : base + XL_DEV, :]
            right[i, :, pl.ds(at, LANES)] = total[base + XL_DEV : base + XL_DEV + rim, :]
            left[i, :, pl.ds(at, LANES)] = total[base + XL_DEV + rim : base + out_lines, :]
        return carry

    lax.fori_loop(0, blocks, move_out, 0)


def whole(count):
    return [pl.BlockSpec(memory_space=pltpu.VMEM)] * count


def send_call(traces, shot_filter, channel_gain, bin_owner, bin_slot, offset_class, owners):
    rows, samples = traces.shape
    width = samples // HALVES + LANES
    per_owner = CAP * HALVES
    return pl.pallas_call(
        send_kernel,
        out_shape=jax.ShapeDtypeStruct((owners * per_owner, width), BF16),
        in_specs=whole(6),
        out_specs=pl.BlockSpec(memory_space=pltpu.VMEM),
        scratch_shapes=[
            pltpu.VMEM((owners * per_owner, HALVES * rows), BF16),
            pltpu.VMEM((HALVES * rows, width), BF16),
        ],
    )(
        traces,
        shot_filter,
        channel_gain.reshape(1, rows),
        bin_owner.reshape(1, rows),
        bin_slot.reshape(1, rows),
        offset_class.reshape(1, rows),
    )


def stack_call(arrived, dip_filter, nmo_start, nmo_weights):
    offsets, samples = nmo_start.shape
    taps_x, taps_t = dip_filter.shape
    begin = 2 * LANES - LANES // 2 - taps_t // 2
    spread = jnp.pad(
        dip_filter[:, ::-1].astype(F32), ((0, 0), (begin, 2 * LANES - begin - taps_t))
    )
    steps = 18
    lines = IL_DEV * offsets
    edge = jax.ShapeDtypeStruct((IL_DEV, XL_DEV // 2, samples), F32)
    return pl.pallas_call(
        stack_kernel,
        out_shape=(jax.ShapeDtypeStruct((IL_DEV, XL_DEV, samples), F32), edge, edge),
        in_specs=whole(4),
        out_specs=tuple(whole(3)),
        scratch_shapes=[
            pltpu.VMEM((steps, lines, 2 * LANES * XL_DEV), BF16),
            pltpu.VMEM(((taps_x + 1) * 2 * LANES, 2 * LANES), BF16),
            pltpu.VMEM((steps, 2 * XL_DEV * lines, LANES), F32),
        ],
    )(arrived, spread, nmo_start, nmo_weights)


def per_device(
    traces,
    shot_filter,
    channel_gain,
    bin_owner,
    bin_slot,
    offset_class,
    dip_filter,
    nmo_start,
    nmo_weights,
):
    owners = lax.axis_size("shot") * lax.axis_size("bin")
    outgoing = send_call(
        traces, shot_filter, channel_gain, bin_owner, bin_slot, offset_class, owners
    )
    rows, width = outgoing.shape
    arrived = lax.all_to_all(
        outgoing.reshape(owners, rows // owners, width), ("shot", "bin"), 0, 0, tiled=True
    ).reshape(rows, width)
    centre, right, left = stack_call(arrived, dip_filter, nmo_start, nmo_weights)
    count = lax.axis_size("bin")
    ends = range(count - 1)
    from_left = lax.ppermute(right, "bin", [(i, i + 1) for i in ends])
    from_right = lax.ppermute(left, "bin", [(i + 1, i) for i in ends])
    return centre + jnp.concatenate([from_left, from_right], axis=1)


def solution(mesh):
    placed = (
        P(("shot", "bin"), None),
        P(("shot", "bin"), None),
        P(),
        P(("shot", "bin"), None),
        P(("shot", "bin")),
        P(("shot", "bin")),
        P(),
        P(),
        P(),
    )
    return jax.shard_map(
        per_device, mesh=mesh, in_specs=placed, out_specs=P("shot", "bin", None), check_vma=False
    )
```

profile of v0, /device:TPU:6, one launch (start us, length us, event | category | flops | bytes accessed | tf_op | source)
XLA Modules:
  0.0 85.1 jit_solution(17872607534955092421)
XLA Ops:
  0.0 4.8 %shard_map.91 = bf16[1024,1152]{1,0:T(8,128)(2,1)} custom-call(bf16[256,2048]{1,0:T(8,128)(2,1)} %traces.1, bf16[1,128]{1,0:T(2,128)(2,1)} %shot_filter.1, f32[1,256]{1,0:T(1,128)} %bitcast.8, s32[1,256]{1,0:T(1,128)} %bitcast.9, s32[1,256]{1,0:T(1,128)} %bitcast.10, s32[1,256]{1,0:T(1,128)} %bitcast.11), custom_call_target="tpu_custom_call" | custom-call | tf_op jit(solution)/shard_map/pallas_call | solution.py:194
  4.8 0.0 copy-start.1
  4.8 10.5 %all-to-all-start = ((bf16[128,8,1152]{2,1,0:T(8,128)(2,1)}), bf16[128,8,1152]{2,1,0:T(8,128)(2,1)S(1)}, u32[]{:S(2)}, u32[]{:S(2)}) async-start(bf16[128,8,1152]{2,1,0:T(8,128)(2,1)} %bitcast.7), calls=%async_computation | async-start | bytes 4718592 | tf_op jit(solution)/shard_map/all_to_all | solution.py:252
  15.3 0.0 copy-done.1
  15.3 0.1 rev.3
  15.4 0.7 pad_convert_fusion.dip
  16.1 31.1 %all-to-all-done = bf16[128,8,1152]{2,1,0:T(8,128)(2,1)S(1)} async-done(((bf16[128,8,1152]{2,1,0:T(8,128)(2,1)}), bf16[128,8,1152]{2,1,0:T(8,128)(2,1)S(1)}, u32[]{:S(2)}, u32[]{:S(2)}) %all-to-all-start) | async-done | bytes 2359328 | tf_op jit(solution)/shard_map/all_to_all | solution.py:252
  47.1 0.0 copy-start
  47.1 1.4 %copy-done = bf16[128,8,1152]{2,1,0:T(8,128)(2,1)} copy-done((bf16[128,8,1152]{2,1,0:T(8,128)(2,1)}, bf16[128,8,1152]{2,1,0:T(8,128)(2,1)S(1)}, u32[]{:S(2)}) %copy-start) | copy-done | bytes 2359320
  48.6 22.9 %shard_map.92 = (f32[2,8,2048]{2,1,0:T(8,128)}, f32[2,4,2048]{2,1,0:T(4,128)}, f32[2,4,2048]{2,1,0:T(4,128)}) custom-call(bf16[1024,1152]{1,0:T(8,128)(2,1)} %bitcast.6, f32[9,256]{1,0:T(8,128)} %pad_convert_fusion.dip, s32[32,2048]{1,0:T(8,128)} %start.1, bf16[32,8,2048]{2,1,0:T(8,128)(2,1)} %weights.1), custom_call_target="tpu_custom_call" | custom-call | tf_op jit(solution)/shard_map/pallas_call | solution.py:223
  71.4 3.6 %collective-permute-start = (f32[2,4,2048]{2,1,0:T(4,128)}, f32[2,4,2048]{2,1,0:T(4,128)S(1)}, u32[]{:S(2)}, u32[]{:S(2)}) collective-permute-start(f32[2,4,2048]{2,1,0:T(4,128)} %get-tuple-element.9), channel_id=1, source_target_pairs={{0,1},{1,2},{2,3},{3,4},{4,5},{5,6},{6,7},{7,8},{8,9},{9,10},{10,1... | collective-permute-start | bytes 196616 | tf_op jit(solution)/shard_map/ppermute | solution.py:258
  75.1 2.2 %collective-permute-start.1 = (f32[2,4,2048]{2,1,0:T(4,128)}, f32[2,4,2048]{2,1,0:T(4,128)S(1)}, u32[]{:S(2)}, u32[]{:S(2)}) collective-permute-start(f32[2,4,2048]{2,1,0:T(4,128)} %get-tuple-element.10), channel_id=1, source_target_pairs={{1,0},{2,1},{3,2},{4,3},{5,4},{6,5},{7,6},{8,7},{9,8},{10,9},{11,1... | collective-permute-start | bytes 196616 | tf_op jit(solution)/shard_map/ppermute | solution.py:259
  77.3 0.6 collective-permute-done
  77.8 5.7 %collective-permute-done.1 = f32[2,4,2048]{2,1,0:T(4,128)S(1)} collective-permute-done((f32[2,4,2048]{2,1,0:T(4,128)}, f32[2,4,2048]{2,1,0:T(4,128)S(1)}, u32[]{:S(2)}, u32[]{:S(2)}) %collective-permute-start.1) | collective-permute-done | bytes 65568 | tf_op jit(solution)/shard_map/ppermute | solution.py:259
  83.5 1.6 %maximum_add_fusion = f32[2,8,2048]{2,1,0:T(8,128)} fusion(f32[2,8,2048]{2,1,0:T(8,128)} %get-tuple-element.8, f32[2,4,2048]{2,1,0:T(4,128)S(1)} %collective-permute-done.1, f32[2,4,2048]{2,1,0:T(4,128)S(1)} %collective-permute-done), kind=kLoop, calls=%fused_computation | loop fusion | flops 65536 | bytes 393216 | tf_op jit(solution)/shard_map/add | solution.py:260
Async XLA Ops:
  4.8 10.5 %copy-start.1 = (bf16[9,31]{1,0:T(8,128)(2,1)S(1)}, bf16[9,31]{1,0:T(8,128)(2,1)}, u32[]{:S(2)}) copy-start(bf16[9,31]{1,0:T(8,128)(2,1)} %param.15) | copy-start | bytes 1678
  4.8 42.3 %all-to-all-start = ((bf16[128,8,1152]{2,1,0:T(8,128)(2,1)}), bf16[128,8,1152]{2,1,0:T(8,128)(2,1)S(1)}, u32[]{:S(2)}, u32[]{:S(2)}) async-start(bf16[128,8,1152]{2,1,0:T(8,128)(2,1)} %bitcast.7), calls=%async_computation | async-start | bytes 4718592 | tf_op jit(solution)/shard_map/all_to_all | solution.py:252
  47.1 1.4 %copy-start = (bf16[128,8,1152]{2,1,0:T(8,128)(2,1)}, bf16[128,8,1152]{2,1,0:T(8,128)(2,1)S(1)}, u32[]{:S(2)}) copy-start(bf16[128,8,1152]{2,1,0:T(8,128)(2,1)S(1)} %all-to-all-done) | copy-start | bytes 7077892
  71.4 6.4 %collective-permute-start = (f32[2,4,2048]{2,1,0:T(4,128)}, f32[2,4,2048]{2,1,0:T(4,128)S(1)}, u32[]{:S(2)}, u32[]{:S(2)}) collective-permute-start(f32[2,4,2048]{2,1,0:T(4,128)} %get-tuple-element.9), channel_id=1, source_target_pairs={{0,1},{1,2},{2,3},{3,4},{4,5},{5,6},{6,7},{7,8},{8,9},{9,10},{10,1... | collective-permute-start | bytes 196616 | tf_op jit(solution)/shard_map/ppermute | solution.py:258
  75.1 8.5 %collective-permute-start.1 = (f32[2,4,2048]{2,1,0:T(4,128)}, f32[2,4,2048]{2,1,0:T(4,128)S(1)}, u32[]{:S(2)}, u32[]{:S(2)}) collective-permute-start(f32[2,4,2048]{2,1,0:T(4,128)} %get-tuple-element.10), channel_id=1, source_target_pairs={{1,0},{2,1},{3,2},{4,3},{5,4},{6,5},{7,6},{8,7},{9,8},{10,9},{11,1... | collective-permute-start | bytes 196616 | tf_op jit(solution)/shard_map/ppermute | solution.py:259
where the time goes:
time: 85.4 us; the launch traced here: 85.1 us
  waiting for transfers between devices  37.4 us (44%)
  Pallas kernels  27.7 us (32%)
  starting transfers between devices  16.3 us (19%)
  other arithmetic  2.27 us (3%)
  local copies, waits for them, and re-layouts  1.5 us (2%)
    all_to_all x1, waiting for transfers between devices, per_device(): lax.all_to_all(outgoing.reshape(owners, rows // owners, width), ('shot',...  31.1 us
    pallas_call x1, Pallas kernels, stack_call(): pl.pallas_call(stack_kernel, out_shape=(jax.ShapeDtypeStruct((IL_DEV, XL_...  22.9 us
    all_to_all x1, starting transfers between devices, per_device(): lax.all_to_all(outgoing.reshape(owners, rows // owners, width), ('shot',...  10.5 us
    ppermute x1, waiting for transfers between devices, per_device(): from_right = lax.ppermute(left, 'bin', [(i + 1, i) for i in ends])  5.7 us
    pallas_call x1, Pallas kernels, send_call(): pl.pallas_call(send_kernel, out_shape=jax.ShapeDtypeStruct((owners * per_...  4.81 us
    ppermute x1, starting transfers between devices, per_device(): from_left = lax.ppermute(right, 'bin', [(i, i + 1) for i in ends])  3.64 us
    ppermute x1, starting transfers between devices, per_device(): from_right = lax.ppermute(left, 'bin', [(i + 1, i) for i in ends])  2.19 us
  transfers between devices with their start and end apart: 3, of which 3 were waited for; matrix products, arithmetic and copies ran while one was open for 1% of the time, Pallas kernels for 0%

commit v1 on v0

--- a/solution.py
+++ b/solution.py
@@ -12,6 +12,9 @@
 XL_DEV = 8
 CAP = 4
 HALVES = 2
+STEPS = 2
+STRIDE = 33
+MERGE = 4
 F32 = jnp.float32
 BF16 = jnp.bfloat16
 
@@ -20,11 +23,29 @@
     return lax.broadcasted_iota(jnp.int32, shape, dim)
 
 
-def send_kernel(traces, shot_filter, gain, owner, slot, offset, out, placed, filtered):
+def woven(first, second):
+    rows, width = first.shape
+    first, second = first.reshape(rows // 8, 8, width), second.reshape(rows // 8, 8, width)
+    low = iota(first.shape, 1) < CAP
+    even = jnp.where(low, first, pltpu.roll(second, CAP, 1))
+    odd = jnp.where(low, pltpu.roll(first, CAP, 1), second)
+    return jnp.stack([even, odd], axis=1).reshape(2 * rows, width)
+
+
+def apart(rows):
+    count, width = rows.shape
+    pairs = rows.astype(F32).reshape(count // 16, 2, 8, width)
+    even, odd = pairs[:, 0], pairs[:, 1]
+    low = iota(even.shape, 1) < CAP
+    first = jnp.where(low, even, pltpu.roll(odd, CAP, 1))
+    second = jnp.where(low, pltpu.roll(even, CAP, 1), odd)
+    return first.reshape(count // 2, width), second.reshape(count // 2, width)
+
+
+def send_kernel(traces, shot_filter, gain, owner, slot, offset, out, filtered):
     rows, samples = traces.shape
     blocks = samples // LANES
     half = samples // HALVES
-    offsets = 32
     slots = slot[...]
     hi = (slots % XL_DEV) * IL_DEV + slots // XL_DEV
     lo = offset[...]
@@ -41,13 +62,8 @@
     owner_row = owner[...]
     same = (owner_column == owner_row) & (iota((rows, rows), 0) < iota((rows, rows), 1))
     rank = jnp.sum(jnp.where(same, 1.0, 0.0), axis=0, keepdims=True).astype(jnp.int32)
-    target = owner_row * (CAP * HALVES) + rank
-    out_rows = out.shape[0]
-    row_ids = iota((out_rows, rows), 0)
-    for h in range(HALVES):
-        placed[:, h * rows : (h + 1) * rows] = jnp.where(
-            row_ids == target + h * CAP, 1.0, 0.0
-        ).astype(BF16)
+    row_ids = iota((out.shape[0] // HALVES, rows), 0)
+    placed = jnp.where(row_ids == owner_row * CAP + rank, 1.0, 0.0).astype(BF16)
     taps = jnp.broadcast_to(shot_filter[...].astype(F32), (LANES, LANES))
     circulant = pltpu.roll(taps, 0, 1, stride=1, stride_axis=0)
     later = iota((LANES, LANES), 0) > iota((LANES, LANES), 1)
@@ -63,17 +79,22 @@
             )
         h, at = divmod(j * LANES, half)
         filtered[h * rows : (h + 1) * rows, at : at + LANES] = (value * gain_column).astype(BF16)
-    for h in range(HALVES):
-        filtered[h * rows : (h + 1) * rows, half:] = codes
     width = 2 * LANES
-    for n in range(0, filtered.shape[1], width):
-        stop = min(n + width, filtered.shape[1])
-        out[:, n:stop] = jnp.dot(
-            placed[...], filtered[:, n:stop], preferred_element_type=F32
-        ).astype(BF16)
-
-
-def stack_kernel(arrived, dip, start, weights, centre, right, left, windows, dips, dipped):
+    for n in range(0, half, width):
+        parts = [
+            jnp.dot(
+                placed,
+                filtered[h * rows : (h + 1) * rows, n : n + width],
+                preferred_element_type=F32,
+            )
+            for h in range(HALVES)
+        ]
+        out[:, n : n + width] = woven(*parts).astype(BF16)
+    part = jnp.dot(placed, codes, preferred_element_type=F32)
+    out[:, half:] = woven(part, part).astype(BF16)
+
+
+def stack_kernel(arrived, dip, start, weights, centre, right, left, binned, dips, dipped):
     slots = arrived.shape[0]
     half = arrived.shape[1] - LANES
     offsets, samples = start.shape
@@ -83,33 +104,27 @@
     taps_x = dip.shape[0]
     rim = XL_DEV // 2
     out_lines = 2 * XL_DEV
-    codes = arrived[:, half:]
-    rows = codes.astype(F32).T
+    codes = apart(arrived[:, half:])[0]
+    rows = codes.T
     code = jnp.where(rows[0:1] > 0.5, rows[1:2] * offsets + rows[2:3], -1.0).astype(jnp.int32)
-    part = (iota((1, slots), 1) // CAP) % HALVES
-    cell_ids = iota((cells, slots), 0)
-    members = []
-    for h in range(HALVES):
-        hit = cell_ids == jnp.where(part == h, code, -1)
-        members.append(jnp.where(hit, 1.0, 0.0).astype(BF16))
-    fold = jnp.dot(members[0], codes, preferred_element_type=F32)[:, 0:1]
+    hit = iota((cells, slots // HALVES), 0) == code
+    member = jnp.where(hit, 1.0, 0.0).astype(BF16)
+    fold = jnp.dot(member, codes.astype(BF16), preferred_element_type=F32)[:, 0:1]
     scale = 1.0 / jnp.maximum(fold, 1.0)
-    zero = jnp.zeros((lines, LANES), BF16)
-    for x in range(XL_DEV):
-        windows[0, :, 2 * x * LANES : (2 * x + 1) * LANES] = zero
-        windows[blocks, :, (2 * x + 1) * LANES : (2 * x + 2) * LANES] = zero
+    zero = jnp.zeros((XL_DEV, lines, LANES), BF16)
+    binned[0] = zero
+    binned[blocks + 1] = zero
     width = 2 * LANES
-    for h in range(HALVES):
-        for n in range(0, half, width):
-            binned = (
-                jnp.dot(members[h], arrived[:, n : n + width], preferred_element_type=F32) * scale
+    for n in range(0, half, width):
+        parts = apart(arrived[:, n : n + width])
+        for h in range(HALVES):
+            value = (
+                jnp.dot(member, parts[h].astype(BF16), preferred_element_type=F32) * scale
             ).astype(BF16)
             for b in range(width // LANES):
-                block = (h * half + n) // LANES + b
-                for x in range(XL_DEV):
-                    piece = binned[x * lines : (x + 1) * lines, b * LANES : (b + 1) * LANES]
-                    windows[block, :, (2 * x + 1) * LANES : (2 * x + 2) * LANES] = piece
-                    windows[block + 1, :, 2 * x * LANES : (2 * x + 1) * LANES] = piece
+                binned[(h * half + n) // LANES + b + 1] = value[
+                    :, b * LANES : (b + 1) * LANES
+                ].reshape(XL_DEV, lines, LANES)
     bands = []
     for a in range(taps_x):
         spread = jnp.broadcast_to(dip[a : a + 1, :], (2 * LANES, 2 * LANES))
@@ -120,7 +135,7 @@
         dips[d * width : (d + 1) * width, :LANES] = bands[d] if d < taps_x else none
         dips[d * width : (d + 1) * width, LANES:] = bands[d - 1] if d > 0 else none
 
-    group = dipped.shape[0] // 3
+    group = dipped.shape[0] // STEPS
 
     def filter_group(g, carry):
         first = g * group
@@ -128,50 +143,61 @@
             low = max(0, 2 * pair - 2 * rim)
             high = min(XL_DEV, 2 * pair + 2)
             d = low - 2 * pair + 2 * rim
-            lhs = windows[pl.ds(first, group), :, low * width : high * width]
+            lhs = jnp.concatenate(
+                [
+                    binned[pl.ds(first + b, group), x].reshape(group * lines, LANES)
+                    for x in range(low, high)
+                    for b in range(2)
+                ],
+                axis=1,
+            )
             value = jnp.dot(
-                lhs.reshape(group * lines, (high - low) * width),
-                dips[d * width : (d + high - low) * width, :],
-                preferred_element_type=F32,
+                lhs, dips[d * width : (d + high - low) * width, :], preferred_element_type=F32
             )
             for m in range(group):
                 for i in range(IL_DEV):
                     for s in range(2):
                         line = (2 * pair + s - rim) % out_lines
                         at = m * lines + i * offsets
-                        dipped[first + m, pl.ds(i * out_lines + line, offsets, stride=2 * out_lines), :] = (
+                        dipped[first + m, pl.ds(i * out_lines + line, offsets, stride=STRIDE), :] = (
                             value[at : at + offsets, s * LANES : (s + 1) * LANES]
                         )
         return carry
 
-    lax.fori_loop(0, 3, filter_group, 0)
+    lax.fori_loop(0, STEPS, filter_group, 0)
 
     tile = 8
-    groups = 2 * LANES // tile
     span = 2 * out_lines
     sublane = iota((tile, LANES), 0)
     root = 1.0 / math.sqrt(offsets)
+    nothing = jnp.zeros((2 * tile, LANES), BF16)
 
     def move_out(j, carry):
         at = pl.multiple_of(j * LANES, LANES)
         firsts = start[:, pl.ds(at, LANES)] + (LANES // 2 - at)
         total = jnp.zeros((span, LANES), F32)
+        lhs, band = [], []
         for o in range(offsets):
             first = jnp.broadcast_to(firsts[o : o + 1, :], (tile, LANES))
-            turned = weights[o, :, pl.ds(at, LANES)].astype(F32)
-            for bit in (1, 2, 4):
-                turned = jnp.where(
-                    (first & bit) != 0, pltpu.roll(turned, bit, 0), turned
+            turned = jnp.take_along_axis(
+                weights[o, :, pl.ds(at, LANES)].astype(F32), (sublane - first) & (tile - 1), axis=0
+            )
+            turned = jnp.concatenate([turned, turned], axis=0).astype(BF16)
+            place = ((first - sublane + (tile - 1)) >> 3).astype(F32)
+            place = jnp.concatenate([place, place - 1.0], axis=0).astype(BF16)
+            band += [
+                jnp.where(place == float(g), turned, nothing)
+                for g in range(0, 2 * LANES // tile, 2)
+            ]
+            rows = pl.ds(o * STRIDE, span)
+            lhs += [dipped[j, rows, :].astype(BF16), dipped[j + 1, rows, :].astype(BF16)]
+            if o % MERGE == MERGE - 1:
+                total = total + jnp.dot(
+                    jnp.concatenate(lhs, axis=1),
+                    jnp.concatenate(band, axis=0),
+                    preferred_element_type=F32,
                 )
-            place = (first - sublane + (tile - 1)) >> 3
-            band = jnp.concatenate(
-                [jnp.where(place == g, turned, 0.0) for g in range(groups)], axis=0
-            ).astype(BF16)
-            rows = pl.ds(o * span, span)
-            lhs = jnp.concatenate(
-                [dipped[j, rows, :].astype(BF16), dipped[j + 1, rows, :].astype(BF16)], axis=1
-            )
-            total = total + jnp.dot(lhs, band, preferred_element_type=F32)
+                lhs, band = [], []
         total = total * root
         for i in range(IL_DEV):
             base = i * out_lines
@@ -197,9 +223,9 @@
         in_specs=whole(6),
         out_specs=pl.BlockSpec(memory_space=pltpu.VMEM),
         scratch_shapes=[
-            pltpu.VMEM((owners * per_owner, HALVES * rows), BF16),
-            pltpu.VMEM((HALVES * rows, width), BF16),
+            pltpu.VMEM((HALVES * rows, samples // HALVES), BF16),
         ],
+        compiler_params=pltpu.CompilerParams(vmem_limit_bytes=16 * 2**20),
     )(
         traces,
         shot_filter,
@@ -217,7 +243,7 @@
     spread = jnp.pad(
         dip_filter[:, ::-1].astype(F32), ((0, 0), (begin, 2 * LANES - begin - taps_t))
     )
-    steps = 18
+    blocks = samples // LANES
     lines = IL_DEV * offsets
     edge = jax.ShapeDtypeStruct((IL_DEV, XL_DEV // 2, samples), F32)
     return pl.pallas_call(
@@ -226,10 +252,11 @@
         in_specs=whole(4),
         out_specs=tuple(whole(3)),
         scratch_shapes=[
-            pltpu.VMEM((steps, lines, 2 * LANES * XL_DEV), BF16),
+            pltpu.VMEM((blocks + 3, XL_DEV, lines, LANES), BF16),
             pltpu.VMEM(((taps_x + 1) * 2 * LANES, 2 * LANES), BF16),
-            pltpu.VMEM((steps, 2 * XL_DEV * lines, LANES), F32),
+            pltpu.VMEM((blocks + 2, offsets * STRIDE, LANES), F32),
         ],
+        compiler_params=pltpu.CompilerParams(vmem_limit_bytes=30 * 2**20),
     )(arrived, spread, nmo_start, nmo_weights)
 
 

time: 85.4 us -> 78.7 us (0.922)
  Pallas kernels: 27.7 us -> 16.4 us
  local copies, waits for them, and re-layouts: 1.5 us -> 7.06 us
  other arithmetic: 2.27 us -> 0.77 us
    pallas_call x1, Pallas kernels: 22.9 us -> 15 us  [stack_call(): pl.pallas_call(stack_kernel, out_shape=(jax.ShapeDtypeStruct((IL_DEV, XL_...]
    unnamed x4 -> x20, local copies, waits for them, and re-layouts: 1.41 us -> 6.97 us
    pallas_call x1, Pallas kernels: 4.81 us -> 1.46 us  [send_call(): pl.pallas_call(send_kernel, out_shape=jax.ShapeDtypeStruct((owners * per_...]
    add x1, other arithmetic: 1.6 us -> 0.69 us  [per_device(): return centre + jnp.concatenate([from_left, from_right], axis=1)]
  transfers between devices with their start and end apart: 3 -> 3, of which waited for: 3 -> 3; matrix products, arithmetic and copies ran while one was open for 1% -> 0% of each run, Pallas kernels for 0% -> 0%
where the time goes in v1:
time: 78.7 us; the launch traced here: 78.4 us
  waiting for transfers between devices  37.7 us (48%)
  Pallas kernels  16.4 us (21%)
  starting transfers between devices  16.3 us (21%)
  local copies, waits for them, and re-layouts  7.06 us (9%)
    all_to_all x1, waiting for transfers between devices, per_device(): lax.all_to_all(outgoing.reshape(owners, rows // owners, width), ('shot',...  31.7 us
    pallas_call x1, Pallas kernels, stack_call(): pl.pallas_call(stack_kernel, out_shape=(jax.ShapeDtypeStruct((IL_DEV, XL_...  15 us
    all_to_all x1, starting transfers between devices, per_device(): lax.all_to_all(outgoing.reshape(owners, rows // owners, width), ('shot',...  10.5 us
    unnamed x20, local copies, waits for them, and re-layouts  6.97 us
    ppermute x1, waiting for transfers between devices, per_device(): from_right = lax.ppermute(left, 'bin', [(i + 1, i) for i in ends])  5.7 us
    ppermute x1, starting transfers between devices, per_device(): from_left = lax.ppermute(right, 'bin', [(i, i + 1) for i in ends])  3.65 us
    ppermute x1, starting transfers between devices, per_device(): from_right = lax.ppermute(left, 'bin', [(i + 1, i) for i in ends])  2.19 us
  transfers between devices with their start and end apart: 3, of which 3 were waited for; matrix products, arithmetic and copies ran while one was open for 0% of the time, Pallas kernels for 0%

profile of v1, /device:TPU:6, one launch (start us, length us, event | category | flops | bytes accessed | tf_op | source)
XLA Modules:
  0.0 78.4 jit_solution(607659398191667289)
XLA Ops:
  0.0 0.0 copy-start.1
  0.0 1.2 %copy-done.1 = bf16[256,2048]{1,0:T(8,128)(2,1)S(1)} copy-done((bf16[256,2048]{1,0:T(8,128)(2,1)S(1)}, bf16[256,2048]{1,0:T(8,128)(2,1)}, u32[]{:S(2)}) %copy-start.1) | copy-done | bytes 1048600
  1.2 0.0 copy-start.4
  1.2 0.7 copy-done.4
  1.9 0.0 copy-start.5
  1.9 0.7 copy-done.5
  2.6 0.0 copy-start.6
  2.6 0.7 copy-done.6
  3.3 0.0 copy-start.7
  3.3 0.7 copy-done.7
  3.9 0.0 copy-start.8
  3.9 0.7 copy-done.8
  4.6 1.5 %shard_map.91 = bf16[1024,1152]{1,0:T(8,128)(2,1)S(1)} custom-call(bf16[256,2048]{1,0:T(8,128)(2,1)S(1)} %copy-done.1, bf16[1,128]{1,0:T(2,128)(2,1)S(1)} %copy-done.8, f32[1,256]{1,0:T(1,128)S(1)} %bitcast.8, s32[1,256]{1,0:T(1,128)S(1)} %bitcast.9, s32[1,256]{1,0:T(1,128)S(1)} %bitcast.10, s32[1,256]{1,0:T(1,128)S(1)} %bitcast.11), custom_call_target="tpu_custom_call" | custom-call | tf_op jit(solution)/shard_map/pallas_call | solution.py:220
  6.1 0.0 copy-start
  6.1 1.4 %copy-done = bf16[1024,1152]{1,0:T(8,128)(2,1)} copy-done((bf16[1024,1152]{1,0:T(8,128)(2,1)}, bf16[1024,1152]{1,0:T(8,128)(2,1)S(1)}, u32[]{:S(2)}) %copy-start) | copy-done | bytes 2359320
  7.5 0.0 copy-start.9
  7.5 0.0 copy-start.2
  7.5 10.5 %all-to-all-start = ((bf16[128,8,1152]{2,1,0:T(8,128)(2,1)}), bf16[128,8,1152]{2,1,0:T(8,128)(2,1)S(1)}, u32[]{:S(2)}, u32[]{:S(2)}) async-start(bf16[128,8,1152]{2,1,0:T(8,128)(2,1)} %bitcast.7), calls=%async_computation | async-start | bytes 4718592 | tf_op jit(solution)/shard_map/all_to_all | solution.py:279
  18.0 0.0 copy-done.9
  18.0 0.1 rev.3
  18.1 0.1 pad_convert_fusion.dip
  18.2 31.7 %all-to-all-done = bf16[128,8,1152]{2,1,0:T(8,128)(2,1)S(1)} async-done(((bf16[128,8,1152]{2,1,0:T(8,128)(2,1)}), bf16[128,8,1152]{2,1,0:T(8,128)(2,1)S(1)}, u32[]{:S(2)}, u32[]{:S(2)}) %all-to-all-start) | async-done | bytes 2359328 | tf_op jit(solution)/shard_map/all_to_all | solution.py:279
  49.8 0.0 copy-done.2
  49.8 0.0 copy-start.3
  49.8 0.9 %copy-done.3 = s32[32,2048]{1,0:T(8,128)S(1)} copy-done((s32[32,2048]{1,0:T(8,128)S(1)}, s32[32,2048]{1,0:T(8,128)}, u32[]{:S(2)}) %copy-start.3) | copy-done | bytes 262168
  50.8 15.0 %shard_map.92 = (f32[2,8,2048]{2,1,0:T(8,128)S(1)}, f32[2,4,2048]{2,1,0:T(4,128)S(1)}, f32[2,4,2048]{2,1,0:T(4,128)S(1)}) custom-call(bf16[1024,1152]{1,0:T(8,128)(2,1)S(1)} %bitcast.6, f32[9,256]{1,0:T(8,128)S(1)} %pad_convert_fusion.dip, s32[32,2048]{1,0:T(8,128)S(1)} %copy-done.3, bf16[32,8,2048]{2,1,0:T(8,128)(2,1)S(1)} %copy-done.2), custom_call_target="tpu_custom_call" | custom-call | tf_op jit(solution)/shard_map/pallas_call | solution.py:249
  65.8 3.7 %collective-permute-start = (f32[2,4,2048]{2,1,0:T(4,128)S(1)}, f32[2,4,2048]{2,1,0:T(4,128)S(1)}, u32[]{:S(2)}, u32[]{:S(2)}) collective-permute-start(f32[2,4,2048]{2,1,0:T(4,128)S(1)} %get-tuple-element.9), channel_id=1, source_target_pairs={{0,1},{1,2},{2,3},{3,4},{4,5},{5,6},{6,7},{7,8},{8,9},{9,10},{10,1... | collective-permute-start | bytes 196616 | tf_op jit(solution)/shard_map/ppermute | solution.py:285
  69.4 2.2 %collective-permute-start.1 = (f32[2,4,2048]{2,1,0:T(4,128)S(1)}, f32[2,4,2048]{2,1,0:T(4,128)S(1)}, u32[]{:S(2)}, u32[]{:S(2)}) collective-permute-start(f32[2,4,2048]{2,1,0:T(4,128)S(1)} %get-tuple-element.10), channel_id=1, source_target_pairs={{1,0},{2,1},{3,2},{4,3},{5,4},{6,5},{7,6},{8,7},{9,8},{10,9},{11,1... | collective-permute-start | bytes 196616 | tf_op jit(solution)/shard_map/ppermute | solution.py:286
  71.6 0.4 collective-permute-done
  72.0 5.7 %collective-permute-done.1 = f32[2,4,2048]{2,1,0:T(4,128)S(1)} collective-permute-done((f32[2,4,2048]{2,1,0:T(4,128)S(1)}, f32[2,4,2048]{2,1,0:T(4,128)S(1)}, u32[]{:S(2)}, u32[]{:S(2)}) %collective-permute-start.1) | collective-permute-done | bytes 65568 | tf_op jit(solution)/shard_map/ppermute | solution.py:286
  77.7 0.7 maximum_add_fusion
Async XLA Ops:
  0.0 1.2 %copy-start.1 = (bf16[256,2048]{1,0:T(8,128)(2,1)S(1)}, bf16[256,2048]{1,0:T(8,128)(2,1)}, u32[]{:S(2)}) copy-start(bf16[256,2048]{1,0:T(8,128)(2,1)} %traces.1) | copy-start | bytes 3145732
  1.2 0.7 copy-start.4
  1.9 0.7 copy-start.5
  2.6 0.7 copy-start.6
  3.3 0.7 copy-start.7
  3.9 0.7 copy-start.8
  6.1 1.4 %copy-start = (bf16[1024,1152]{1,0:T(8,128)(2,1)}, bf16[1024,1152]{1,0:T(8,128)(2,1)S(1)}, u32[]{:S(2)}) copy-start(bf16[1024,1152]{1,0:T(8,128)(2,1)S(1)} %shard_map.91) | copy-start | bytes 7077892
  7.5 10.5 %copy-start.9 = (bf16[9,31]{1,0:T(8,128)(2,1)S(1)}, bf16[9,31]{1,0:T(8,128)(2,1)}, u32[]{:S(2)}) copy-start(bf16[9,31]{1,0:T(8,128)(2,1)} %param.15) | copy-start | bytes 1678
  7.5 42.3 %copy-start.2 = (bf16[32,8,2048]{2,1,0:T(8,128)(2,1)S(1)}, bf16[32,8,2048]{2,1,0:T(8,128)(2,1)}, u32[]{:S(2)}) copy-start(bf16[32,8,2048]{2,1,0:T(8,128)(2,1)} %weights.1) | copy-start | bytes 3145732
  7.5 42.3 %all-to-all-start = ((bf16[128,8,1152]{2,1,0:T(8,128)(2,1)}), bf16[128,8,1152]{2,1,0:T(8,128)(2,1)S(1)}, u32[]{:S(2)}, u32[]{:S(2)}) async-start(bf16[128,8,1152]{2,1,0:T(8,128)(2,1)} %bitcast.7), calls=%async_computation | async-start | bytes 4718592 | tf_op jit(solution)/shard_map/all_to_all | solution.py:279
  49.8 1.0 %copy-start.3 = (s32[32,2048]{1,0:T(8,128)S(1)}, s32[32,2048]{1,0:T(8,128)}, u32[]{:S(2)}) copy-start(s32[32,2048]{1,0:T(8,128)} %start.1) | copy-start | bytes 786436
  65.8 6.2 %collective-permute-start = (f32[2,4,2048]{2,1,0:T(4,128)S(1)}, f32[2,4,2048]{2,1,0:T(4,128)S(1)}, u32[]{:S(2)}, u32[]{:S(2)}) collective-permute-start(f32[2,4,2048]{2,1,0:T(4,128)S(1)} %get-tuple-element.9), channel_id=1, source_target_pairs={{0,1},{1,2},{2,3},{3,4},{4,5},{5,6},{6,7},{7,8},{8,9},{9,10},{10,1... | collective-permute-start | bytes 196616 | tf_op jit(solution)/shard_map/ppermute | solution.py:285
  69.4 8.3 %collective-permute-start.1 = (f32[2,4,2048]{2,1,0:T(4,128)S(1)}, f32[2,4,2048]{2,1,0:T(4,128)S(1)}, u32[]{:S(2)}, u32[]{:S(2)}) collective-permute-start(f32[2,4,2048]{2,1,0:T(4,128)S(1)} %get-tuple-element.10), channel_id=1, source_target_pairs={{1,0},{2,1},{3,2},{4,3},{5,4},{6,5},{7,6},{8,7},{9,8},{10,9},{11,1... | collective-permute-start | bytes 196616 | tf_op jit(solution)/shard_map/ppermute | solution.py:286

commit v2 on v1

--- a/solution.py
+++ b/solution.py
@@ -14,6 +14,8 @@
 HALVES = 2
 STEPS = 2
 STRIDE = 33
+TAIL = 32
+DIP_REACH = 15
 MERGE = 4
 F32 = jnp.float32
 BF16 = jnp.bfloat16
@@ -42,10 +44,24 @@
     return first.reshape(count // 2, width), second.reshape(count // 2, width)
 
 
-def send_kernel(traces, shot_filter, gain, owner, slot, offset, out, filtered):
+def send_kernel(
+    traces_hbm, shot_filter, gain, owner, slot, offset, out_hbm, traces, out, filtered, sems
+):
     rows, samples = traces.shape
     blocks = samples // LANES
     half = samples // HALVES
+    fetch = pltpu.make_async_copy(traces_hbm, traces, sems.at[0])
+    fetch.start()
+    copies = []
+
+    def send(n, stop):
+        columns = (slice(None), slice(n, stop))
+        copy = pltpu.make_async_copy(
+            out.at[columns], out_hbm.at[columns], sems.at[1 + len(copies)]
+        )
+        copy.start()
+        copies.append(copy)
+
     slots = slot[...]
     hi = (slots % XL_DEV) * IL_DEV + slots // XL_DEV
     lo = offset[...]
@@ -70,6 +86,10 @@
     before = jnp.where(later, circulant, 0.0).astype(BF16)
     centre = jnp.where(later, 0.0, circulant).astype(BF16)
     matrix = jnp.concatenate([before, centre], axis=0)
+    part = jnp.dot(placed, codes, preferred_element_type=F32)
+    out[:, half:] = woven(part, part).astype(BF16)
+    send(half, half + LANES)
+    fetch.wait()
     for j in range(blocks):
         if j == 0:
             value = jnp.dot(traces[:, :LANES], centre, preferred_element_type=F32)
@@ -90,18 +110,55 @@
             for h in range(HALVES)
         ]
         out[:, n : n + width] = woven(*parts).astype(BF16)
-    part = jnp.dot(placed, codes, preferred_element_type=F32)
-    out[:, half:] = woven(part, part).astype(BF16)
-
-
-def stack_kernel(arrived, dip, start, weights, centre, right, left, binned, dips, dipped):
+        send(n, n + width)
+    for copy in copies:
+        copy.wait()
+
+
+def prepare_kernel(dip, start, weights, heads, tails, turned, place):
+    taps_x = dip.shape[0]
+    offsets, samples = start.shape
+    bands = []
+    for a in range(taps_x):
+        spread = jnp.broadcast_to(dip[a : a + 1, :], (LANES + TAIL, 2 * LANES))
+        bands.append(pltpu.roll(spread, 1, 1, stride=1, stride_axis=0)[:, :LANES].astype(BF16))
+    none = jnp.zeros((LANES + TAIL, LANES), BF16)
+    for d in range(-2, taps_x + 3):
+        pair = [bands[a] if 0 <= a < taps_x else none for a in (d, d - 1)]
+        for s in range(2):
+            lanes = slice(s * LANES, (s + 1) * LANES)
+            if 0 <= d <= taps_x:
+                heads[d * LANES : (d + 1) * LANES, lanes] = pair[s][:LANES]
+            tails[(d + 2) * TAIL : (d + 3) * TAIL, lanes] = pair[s][LANES:]
+    tile = 8
+    sublane = iota((tile, LANES), 0)
+
+    def offset_bands(j, carry):
+        at = pl.multiple_of(j * LANES, LANES)
+        firsts = start[:, pl.ds(at, LANES)] + (LANES - DIP_REACH - at)
+        for o in range(offsets):
+            first = jnp.broadcast_to(firsts[o : o + 1, :], (tile, LANES))
+            weight = jnp.take_along_axis(
+                weights[o, :, pl.ds(at, LANES)].astype(F32), (sublane - first) & (tile - 1), axis=0
+            )
+            group = ((first - sublane + (tile - 1)) >> 3).astype(F32)
+            rows = slice(o * tile, (o + 1) * tile)
+            turned[j, rows, :] = weight
+            place[j, rows, :] = group
+        return carry
+
+    lax.fori_loop(0, samples // LANES, offset_bands, 0)
+
+
+def stack_kernel(
+    arrived, heads, tails, turned, place, centre, right, left, binned, ends, dipped
+):
     slots = arrived.shape[0]
     half = arrived.shape[1] - LANES
-    offsets, samples = start.shape
-    blocks = samples // LANES
+    blocks = turned.shape[0]
+    offsets = turned.shape[1] // 8
     lines = IL_DEV * offsets
     cells = XL_DEV * lines
-    taps_x = dip.shape[0]
     rim = XL_DEV // 2
     out_lines = 2 * XL_DEV
     codes = apart(arrived[:, half:])[0]
@@ -111,84 +168,79 @@
     member = jnp.where(hit, 1.0, 0.0).astype(BF16)
     fold = jnp.dot(member, codes.astype(BF16), preferred_element_type=F32)[:, 0:1]
     scale = 1.0 / jnp.maximum(fold, 1.0)
-    zero = jnp.zeros((XL_DEV, lines, LANES), BF16)
-    binned[0] = zero
-    binned[blocks + 1] = zero
+    binned[0] = jnp.zeros((XL_DEV, lines, LANES), BF16)
+    binned[blocks + 1] = jnp.zeros((XL_DEV, lines, LANES), BF16)
+    ends[blocks + 1] = jnp.zeros((2, lines, LANES), BF16)
     width = 2 * LANES
+    lane = iota((lines, LANES), 1)
     for n in range(0, half, width):
         parts = apart(arrived[:, n : n + width])
         for h in range(HALVES):
             value = (
                 jnp.dot(member, parts[h].astype(BF16), preferred_element_type=F32) * scale
-            ).astype(BF16)
+            )
             for b in range(width // LANES):
-                binned[(h * half + n) // LANES + b + 1] = value[
-                    :, b * LANES : (b + 1) * LANES
-                ].reshape(XL_DEV, lines, LANES)
-    bands = []
-    for a in range(taps_x):
-        spread = jnp.broadcast_to(dip[a : a + 1, :], (2 * LANES, 2 * LANES))
-        band = pltpu.roll(spread, 0, 1, stride=1, stride_axis=0)
-        bands.append(band[:, :LANES].astype(BF16))
-    none = jnp.zeros((2 * LANES, LANES), BF16)
-    for d in range(taps_x + 1):
-        dips[d * width : (d + 1) * width, :LANES] = bands[d] if d < taps_x else none
-        dips[d * width : (d + 1) * width, LANES:] = bands[d - 1] if d > 0 else none
+                at = (h * half + n) // LANES + b + 1
+                block = value[:, b * LANES : (b + 1) * LANES]
+                binned[at] = block.astype(BF16).reshape(XL_DEV, lines, LANES)
+                for g in range(2):
+                    end = block[g * rim * lines : (g * rim + 1) * lines]
+                    for x in range(1, rim):
+                        line = block[(g * rim + x) * lines : (g * rim + x + 1) * lines]
+                        end = jnp.where(lane < x * TAIL, end, pltpu.roll(line, x * TAIL, 1))
+                    ends[at, g] = end.astype(BF16)
 
     group = dipped.shape[0] // STEPS
 
-    def filter_group(g, carry):
-        first = g * group
+    def filter_group(step, carry):
+        first = step * group
         for pair in range(out_lines // 2):
             low = max(0, 2 * pair - 2 * rim)
             high = min(XL_DEV, 2 * pair + 2)
             d = low - 2 * pair + 2 * rim
-            lhs = jnp.concatenate(
-                [
-                    binned[pl.ds(first + b, group), x].reshape(group * lines, LANES)
-                    for x in range(low, high)
-                    for b in range(2)
-                ],
-                axis=1,
-            )
+            lhs = [
+                binned[pl.ds(first, group), x].reshape(group * lines, LANES)
+                for x in range(low, high)
+            ]
+            rhs = [heads[d * LANES : (d + high - low) * LANES, :]]
+            for g in range(2):
+                if low < (g + 1) * rim and high > g * rim:
+                    d = g * rim - 2 * pair + 2 * rim + 2
+                    lhs.append(ends[pl.ds(first + 1, group), g].reshape(group * lines, LANES))
+                    rhs.append(tails[d * TAIL : (d + rim) * TAIL, :])
             value = jnp.dot(
-                lhs, dips[d * width : (d + high - low) * width, :], preferred_element_type=F32
+                jnp.concatenate(lhs, axis=1),
+                jnp.concatenate(rhs, axis=0),
+                preferred_element_type=F32,
             )
             for m in range(group):
                 for i in range(IL_DEV):
                     for s in range(2):
                         line = (2 * pair + s - rim) % out_lines
                         at = m * lines + i * offsets
-                        dipped[first + m, pl.ds(i * out_lines + line, offsets, stride=STRIDE), :] = (
-                            value[at : at + offsets, s * LANES : (s + 1) * LANES]
-                        )
+                        to = pl.ds(i * out_lines + line, offsets, stride=STRIDE)
+                        dipped[first + m, to, :] = value[
+                            at : at + offsets, s * LANES : (s + 1) * LANES
+                        ]
         return carry
 
     lax.fori_loop(0, STEPS, filter_group, 0)
 
+    span = 2 * out_lines
+    root = 1.0 / math.sqrt(offsets)
     tile = 8
-    span = 2 * out_lines
-    sublane = iota((tile, LANES), 0)
-    root = 1.0 / math.sqrt(offsets)
     nothing = jnp.zeros((2 * tile, LANES), BF16)
 
     def move_out(j, carry):
         at = pl.multiple_of(j * LANES, LANES)
-        firsts = start[:, pl.ds(at, LANES)] + (LANES // 2 - at)
         total = jnp.zeros((span, LANES), F32)
         lhs, band = [], []
         for o in range(offsets):
-            first = jnp.broadcast_to(firsts[o : o + 1, :], (tile, LANES))
-            turned = jnp.take_along_axis(
-                weights[o, :, pl.ds(at, LANES)].astype(F32), (sublane - first) & (tile - 1), axis=0
-            )
-            turned = jnp.concatenate([turned, turned], axis=0).astype(BF16)
-            place = ((first - sublane + (tile - 1)) >> 3).astype(F32)
-            place = jnp.concatenate([place, place - 1.0], axis=0).astype(BF16)
-            band += [
-                jnp.where(place == float(g), turned, nothing)
-                for g in range(0, 2 * LANES // tile, 2)
-            ]
+            weight = turned[j, o * tile : (o + 1) * tile, :]
+            weight = jnp.concatenate([weight, weight], axis=0).astype(BF16)
+            group = place[j, o * tile : (o + 1) * tile, :]
+            group = jnp.concatenate([group, group - 1.0], axis=0).astype(BF16)
+            band += [jnp.where(group == float(g), weight, nothing) for g in range(0, 32, 2)]
             rows = pl.ds(o * STRIDE, span)
             lhs += [dipped[j, rows, :].astype(BF16), dipped[j + 1, rows, :].astype(BF16)]
             if o % MERGE == MERGE - 1:
@@ -201,9 +253,10 @@
         total = total * root
         for i in range(IL_DEV):
             base = i * out_lines
+            edge = pl.ds(i * rim, rim)
             centre[i, :, pl.ds(at, LANES)] = total[base : base + XL_DEV, :]
-            right[i, :, pl.ds(at, LANES)] = total[base + XL_DEV : base + XL_DEV + rim, :]
-            left[i, :, pl.ds(at, LANES)] = total[base + XL_DEV + rim : base + out_lines, :]
+            right[edge, pl.ds(at, LANES)] = total[base + XL_DEV : base + XL_DEV + rim, :]
+            left[edge, pl.ds(at, LANES)] = total[base + XL_DEV + rim : base + out_lines, :]
         return carry
 
     lax.fori_loop(0, blocks, move_out, 0)
@@ -220,12 +273,14 @@
     return pl.pallas_call(
         send_kernel,
         out_shape=jax.ShapeDtypeStruct((owners * per_owner, width), BF16),
-        in_specs=whole(6),
-        out_specs=pl.BlockSpec(memory_space=pltpu.VMEM),
+        in_specs=[pl.BlockSpec(memory_space=pl.ANY)] + whole(5),
+        out_specs=pl.BlockSpec(memory_space=pl.ANY),
         scratch_shapes=[
+            pltpu.VMEM((rows, samples), BF16),
+            pltpu.VMEM((owners * per_owner, width), BF16),
             pltpu.VMEM((HALVES * rows, samples // HALVES), BF16),
+            pltpu.SemaphoreType.DMA((2 + samples // HALVES // (2 * LANES),)),
         ],
-        compiler_params=pltpu.CompilerParams(vmem_limit_bytes=16 * 2**20),
     )(
         traces,
         shot_filter,
@@ -236,28 +291,43 @@
     )
 
 
-def stack_call(arrived, dip_filter, nmo_start, nmo_weights):
+def prepare_call(dip_filter, nmo_start, nmo_weights):
     offsets, samples = nmo_start.shape
     taps_x, taps_t = dip_filter.shape
-    begin = 2 * LANES - LANES // 2 - taps_t // 2
-    spread = jnp.pad(
-        dip_filter[:, ::-1].astype(F32), ((0, 0), (begin, 2 * LANES - begin - taps_t))
-    )
-    blocks = samples // LANES
+    spread = jnp.pad(dip_filter[:, ::-1].astype(F32), ((0, 0), (2 * LANES - taps_t, 0)))
+    band = jax.ShapeDtypeStruct((samples // LANES, offsets * 8, LANES), F32)
+    return pl.pallas_call(
+        prepare_kernel,
+        out_shape=(
+            jax.ShapeDtypeStruct(((taps_x + 1) * LANES, 2 * LANES), BF16),
+            jax.ShapeDtypeStruct(((taps_x + 5) * TAIL, 2 * LANES), BF16),
+            band,
+            band,
+        ),
+        in_specs=whole(3),
+        out_specs=tuple(whole(4)),
+        compiler_params=pltpu.CompilerParams(vmem_limit_bytes=20 * 2**20),
+    )(spread, nmo_start, nmo_weights)
+
+
+def stack_call(arrived, heads, tails, turned, place):
+    blocks = turned.shape[0]
+    offsets = turned.shape[1] // 8
+    samples = blocks * LANES
     lines = IL_DEV * offsets
-    edge = jax.ShapeDtypeStruct((IL_DEV, XL_DEV // 2, samples), F32)
+    edge = jax.ShapeDtypeStruct((IL_DEV * XL_DEV // 2, samples), F32)
     return pl.pallas_call(
         stack_kernel,
         out_shape=(jax.ShapeDtypeStruct((IL_DEV, XL_DEV, samples), F32), edge, edge),
-        in_specs=whole(4),
+        in_specs=whole(5),
         out_specs=tuple(whole(3)),
         scratch_shapes=[
-            pltpu.VMEM((blocks + 3, XL_DEV, lines, LANES), BF16),
-            pltpu.VMEM(((taps_x + 1) * 2 * LANES, 2 * LANES), BF16),
+            pltpu.VMEM((blocks + 2, XL_DEV, lines, LANES), BF16),
+            pltpu.VMEM((blocks + 3, 2, lines, LANES), BF16),
             pltpu.VMEM((blocks + 2, offsets * STRIDE, LANES), F32),
         ],
         compiler_params=pltpu.CompilerParams(vmem_limit_bytes=30 * 2**20),
-    )(arrived, spread, nmo_start, nmo_weights)
+    )(arrived, heads, tails, turned, place)
 
 
 def per_device(
@@ -279,12 +349,16 @@
     arrived = lax.all_to_all(
         outgoing.reshape(owners, rows // owners, width), ("shot", "bin"), 0, 0, tiled=True
     ).reshape(rows, width)
-    centre, right, left = stack_call(arrived, dip_filter, nmo_start, nmo_weights)
+    prepared = prepare_call(dip_filter, nmo_start, nmo_weights)
+    centre, right, left = stack_call(arrived, *prepared)
     count = lax.axis_size("bin")
     ends = range(count - 1)
     from_left = lax.ppermute(right, "bin", [(i, i + 1) for i in ends])
     from_right = lax.ppermute(left, "bin", [(i + 1, i) for i in ends])
-    return centre + jnp.concatenate([from_left, from_right], axis=1)
+    shape = (IL_DEV, XL_DEV // 2, centre.shape[2])
+    return centre + jnp.concatenate(
+        [from_left.reshape(shape), from_right.reshape(shape)], axis=1
+    )
 
 
 def solution(mesh):

time: 78.7 us -> 77.9 us (0.990)
  waiting for transfers between devices: 37.7 us -> 31.3 us
  local copies, waits for them, and re-layouts: 7.06 us -> 10.5 us
  Pallas kernels: 16.4 us -> 18.5 us
    all_to_all x1, waiting for transfers between devices: 31.7 us -> 25.2 us  [per_device(): lax.all_to_all(outgoing.reshape(owners, rows // owners, width), ('shot',...]
    unnamed x20 -> x22, local copies, waits for them, and re-layouts: 6.97 us -> 10.4 us
    pallas_call x1, Pallas kernels: 1.46 us -> 4.33 us  [send_call(): pl.pallas_call(send_kernel, out_shape=jax.ShapeDtypeStruct((owners * per_...]
    pallas_call x1, Pallas kernels: 15 us -> 13 us  [stack_call(): pl.pallas_call(stack_kernel, out_shape=(jax.ShapeDtypeStruct((IL_DEV, XL_...]
    pallas_call x0 -> x1, Pallas kernels: none -> 1.24 us  [prepare_call(): pl.pallas_call(prepare_kernel, out_shape=(jax.ShapeDtypeStruct(((taps_x +...]
  transfers between devices with their start and end apart: 3 -> 3, of which waited for: 3 -> 3; matrix products, arithmetic and copies ran while one was open for 0% -> 0% of each run, Pallas kernels for 0% -> 2%
where the time goes in v2:
time: 77.9 us; the launch traced here: 77.5 us
  waiting for transfers between devices  31.3 us (40%)
  Pallas kernels  18.5 us (24%)
  starting transfers between devices  16.3 us (21%)
  local copies, waits for them, and re-layouts  10.5 us (13%)
    all_to_all x1, waiting for transfers between devices, per_device(): lax.all_to_all(outgoing.reshape(owners, rows // owners, width), ('shot',...  25.2 us
    pallas_call x1, Pallas kernels, stack_call(): pl.pallas_call(stack_kernel, out_shape=(jax.ShapeDtypeStruct((IL_DEV, XL_...  13 us
    all_to_all x1, starting transfers between devices, per_device(): lax.all_to_all(outgoing.reshape(owners, rows // owners, width), ('shot',...  10.5 us
    unnamed x22, local copies, waits for them, and re-layouts  10.4 us
    ppermute x1, waiting for transfers between devices, per_device(): from_right = lax.ppermute(left, 'bin', [(i + 1, i) for i in ends])  5.67 us
    pallas_call x1, Pallas kernels, send_call(): pl.pallas_call(send_kernel, out_shape=jax.ShapeDtypeStruct((owners * per_...  4.33 us
    ppermute x1, starting transfers between devices, per_device(): from_left = lax.ppermute(right, 'bin', [(i, i + 1) for i in ends])  3.65 us
    ppermute x1, starting transfers between devices, per_device(): from_right = lax.ppermute(left, 'bin', [(i + 1, i) for i in ends])  2.19 us
  transfers between devices with their start and end apart: 3, of which 3 were waited for; matrix products, arithmetic and copies ran while one was open for 0% of the time, Pallas kernels for 2%

profile of v2, /device:TPU:6, one launch (start us, length us, event | category | flops | bytes accessed | tf_op | source)
XLA Modules:
  0.0 77.5 jit_solution(16033228919002227110)
XLA Ops:
  0.0 4.3 %shard_map.91 = bf16[1024,1152]{1,0:T(8,128)(2,1)} custom-call(bf16[256,2048]{1,0:T(8,128)(2,1)} %traces_hbm.1, bf16[1,128]{1,0:T(2,128)(2,1)} %shot_filter.1, f32[1,256]{1,0:T(1,128)} %bitcast.8, s32[1,256]{1,0:T(1,128)} %bitcast.9, s32[1,256]{1,0:T(1,128)} %bitcast.10, s32[1,256]{1,0:T(1,128)} %bitcast.11), custom_call_target="tpu_custom_call" | custom-call | tf_op jit(solution)/shard_map/pallas_call | solution.py:273
  4.3 0.0 copy-start.10
  4.3 0.0 copy-start.4
  4.4 10.5 %all-to-all-start = ((bf16[128,8,1152]{2,1,0:T(8,128)(2,1)}), bf16[128,8,1152]{2,1,0:T(8,128)(2,1)S(1)}, u32[]{:S(2)}, u32[]{:S(2)}) async-start(bf16[128,8,1152]{2,1,0:T(8,128)(2,1)} %bitcast.7), calls=%async_computation | async-start | bytes 4718592 | tf_op jit(solution)/shard_map/all_to_all | solution.py:349
  14.8 0.0 copy-done.10
  14.9 0.1 rev.3
  14.9 0.1 pad_convert_fusion.dip
  15.0 0.0 copy-done.4
  15.0 0.0 copy-start.7
  15.0 0.9 %copy-done.7 = s32[32,2048]{1,0:T(8,128)S(1)} copy-done((s32[32,2048]{1,0:T(8,128)S(1)}, s32[32,2048]{1,0:T(8,128)}, u32[]{:S(2)}) %copy-start.7) | copy-done | bytes 262168
  16.0 1.2 %shard_map.92 = (bf16[1280,256]{1,0:T(8,128)(2,1)S(1)}, bf16[448,256]{1,0:T(8,128)(2,1)S(1)}, f32[16,256,128]{2,1,0:T(8,128)S(1)}, f32[16,256,128]{2,1,0:T(8,128)S(1)}) custom-call(f32[9,256]{1,0:T(8,128)S(1)} %pad_convert_fusion.dip, s32[32,2048]{1,0:T(8,128)S(1)} %copy-done.7, bf16[32,8,2048]{2,1,0:T(8,128)(2,1)S(1)} %copy-done.4), custom_call_target="tpu_custom_call" | custom-call | tf_op jit(solution)/shard_map/pallas_call | solution.py:299
  17.2 0.0 copy-start
  17.2 1.3 %copy-done = f32[16,256,128]{2,1,0:T(8,128)} copy-done((f32[16,256,128]{2,1,0:T(8,128)}, f32[16,256,128]{2,1,0:T(8,128)S(1)}, u32[]{:S(2)}) %copy-start) | copy-done | bytes 2097176
  18.6 0.0 copy-start.2
  18.6 1.4 %copy-done.2 = f32[16,256,128]{2,1,0:T(8,128)} copy-done((f32[16,256,128]{2,1,0:T(8,128)}, f32[16,256,128]{2,1,0:T(8,128)S(1)}, u32[]{:S(2)}) %copy-start.2) | copy-done | bytes 2097176
  19.9 0.0 copy-start.5
  19.9 0.8 %copy-done.5 = bf16[1280,256]{1,0:T(8,128)(2,1)} copy-done((bf16[1280,256]{1,0:T(8,128)(2,1)}, bf16[1280,256]{1,0:T(8,128)(2,1)S(1)}, u32[]{:S(2)}) %copy-start.5) | copy-done | bytes 655384
  20.8 0.0 copy-start.8
  20.8 0.7 copy-done.8
  21.5 25.2 %all-to-all-done = bf16[128,8,1152]{2,1,0:T(8,128)(2,1)S(1)} async-done(((bf16[128,8,1152]{2,1,0:T(8,128)(2,1)}), bf16[128,8,1152]{2,1,0:T(8,128)(2,1)S(1)}, u32[]{:S(2)}, u32[]{:S(2)}) %all-to-all-start) | async-done | bytes 2359328 | tf_op jit(solution)/shard_map/all_to_all | solution.py:349
  46.7 0.0 copy-start.1
  46.7 1.6 %copy-done.1 = f32[16,256,128]{2,1,0:T(8,128)S(1)} copy-done((f32[16,256,128]{2,1,0:T(8,128)S(1)}, f32[16,256,128]{2,1,0:T(8,128)}, u32[]{:S(2)}) %copy-start.1) | copy-done | bytes 2097176
  48.3 0.0 copy-start.3
  48.3 1.6 %copy-done.3 = f32[16,256,128]{2,1,0:T(8,128)S(1)} copy-done((f32[16,256,128]{2,1,0:T(8,128)S(1)}, f32[16,256,128]{2,1,0:T(8,128)}, u32[]{:S(2)}) %copy-start.3) | copy-done | bytes 2097176
  49.9 0.0 copy-start.6
  49.9 1.1 %copy-done.6 = bf16[1280,256]{1,0:T(8,128)(2,1)S(1)} copy-done((bf16[1280,256]{1,0:T(8,128)(2,1)S(1)}, bf16[1280,256]{1,0:T(8,128)(2,1)}, u32[]{:S(2)}) %copy-start.6) | copy-done | bytes 655384
  51.0 0.0 copy-start.9
  51.0 0.9 %copy-done.9 = bf16[448,256]{1,0:T(8,128)(2,1)S(1)} copy-done((bf16[448,256]{1,0:T(8,128)(2,1)S(1)}, bf16[448,256]{1,0:T(8,128)(2,1)}, u32[]{:S(2)}) %copy-start.9) | copy-done | bytes 229400
  51.9 13.0 %shard_map.93 = (f32[2,8,2048]{2,1,0:T(8,128)S(1)}, f32[8,2048]{1,0:T(8,128)S(1)}, f32[8,2048]{1,0:T(8,128)S(1)}) custom-call(bf16[1024,1152]{1,0:T(8,128)(2,1)S(1)} %bitcast.6, bf16[1280,256]{1,0:T(8,128)(2,1)S(1)} %copy-done.6, bf16[448,256]{1,0:T(8,128)(2,1)S(1)} %copy-done.9, f32[16,256,128]{2,1,0:T(8,128)S(1)} %copy-done.1, f32[16,256,128]{2,1,0:T(8,128)S(1)} %copy-done.3), custom_call_target="tpu_custom_call" | custom-call | tf_op jit(solution)/shard_map/pallas_call | solution.py:319
  64.9 3.7 %collective-permute-start = (f32[8,2048]{1,0:T(8,128)S(1)}, f32[8,2048]{1,0:T(8,128)S(1)}, u32[]{:S(2)}, u32[]{:S(2)}) collective-permute-start(f32[8,2048]{1,0:T(8,128)S(1)} %get-tuple-element.17), channel_id=1, source_target_pairs={{0,1},{1,2},{2,3},{3,4},{4,5},{5,6},{6,7},{7,8},{8,9},{9,10},{10,1... | collective-permute-start | bytes 196616 | tf_op jit(solution)/shard_map/ppermute | solution.py:356
  68.5 2.2 %collective-permute-start.1 = (f32[8,2048]{1,0:T(8,128)S(1)}, f32[8,2048]{1,0:T(8,128)S(1)}, u32[]{:S(2)}, u32[]{:S(2)}) collective-permute-start(f32[8,2048]{1,0:T(8,128)S(1)} %get-tuple-element.18), channel_id=1, source_target_pairs={{1,0},{2,1},{3,2},{4,3},{5,4},{6,5},{7,6},{8,7},{9,8},{10,9},{11,1... | collective-permute-start | bytes 196616 | tf_op jit(solution)/shard_map/ppermute | solution.py:357
  70.7 0.4 collective-permute-done
  71.1 5.7 %collective-permute-done.1 = f32[8,2048]{1,0:T(8,128)S(1)} collective-permute-done((f32[8,2048]{1,0:T(8,128)S(1)}, f32[8,2048]{1,0:T(8,128)S(1)}, u32[]{:S(2)}, u32[]{:S(2)}) %collective-permute-start.1) | collective-permute-done | bytes 65568 | tf_op jit(solution)/shard_map/ppermute | solution.py:357
  76.8 0.7 maximum_add_fusion
  (2 shorter events, 0.0 us)
Async XLA Ops:
  4.3 10.5 %copy-start.10 = (bf16[9,31]{1,0:T(8,128)(2,1)S(1)}, bf16[9,31]{1,0:T(8,128)(2,1)}, u32[]{:S(2)}) copy-start(bf16[9,31]{1,0:T(8,128)(2,1)} %param.15) | copy-start | bytes 1678
  4.3 10.7 %copy-start.4 = (bf16[32,8,2048]{2,1,0:T(8,128)(2,1)S(1)}, bf16[32,8,2048]{2,1,0:T(8,128)(2,1)}, u32[]{:S(2)}) copy-start(bf16[32,8,2048]{2,1,0:T(8,128)(2,1)} %weights.1) | copy-start | bytes 3145732
  4.4 42.3 %all-to-all-start = ((bf16[128,8,1152]{2,1,0:T(8,128)(2,1)}), bf16[128,8,1152]{2,1,0:T(8,128)(2,1)S(1)}, u32[]{:S(2)}, u32[]{:S(2)}) async-start(bf16[128,8,1152]{2,1,0:T(8,128)(2,1)} %bitcast.7), calls=%async_computation | async-start | bytes 4718592 | tf_op jit(solution)/shard_map/all_to_all | solution.py:349
  15.0 1.0 %copy-start.7 = (s32[32,2048]{1,0:T(8,128)S(1)}, s32[32,2048]{1,0:T(8,128)}, u32[]{:S(2)}) copy-start(s32[32,2048]{1,0:T(8,128)} %start.1) | copy-start | bytes 786436
  17.2 1.3 %copy-start = (f32[16,256,128]{2,1,0:T(8,128)}, f32[16,256,128]{2,1,0:T(8,128)S(1)}, u32[]{:S(2)}) copy-start(f32[16,256,128]{2,1,0:T(8,128)S(1)} %get-tuple-element.14.turned) | copy-start | bytes 6291460
  18.6 1.4 %copy-start.2 = (f32[16,256,128]{2,1,0:T(8,128)}, f32[16,256,128]{2,1,0:T(8,128)S(1)}, u32[]{:S(2)}) copy-start(f32[16,256,128]{2,1,0:T(8,128)S(1)} %get-tuple-element.15.place) | copy-start | bytes 6291460
  19.9 0.8 %copy-start.5 = (bf16[1280,256]{1,0:T(8,128)(2,1)}, bf16[1280,256]{1,0:T(8,128)(2,1)S(1)}, u32[]{:S(2)}) copy-start(bf16[1280,256]{1,0:T(8,128)(2,1)S(1)} %get-tuple-element.12.heads) | copy-start | bytes 1966084
  20.8 0.7 copy-start.8
  46.7 1.6 %copy-start.1 = (f32[16,256,128]{2,1,0:T(8,128)S(1)}, f32[16,256,128]{2,1,0:T(8,128)}, u32[]{:S(2)}) copy-start(f32[16,256,128]{2,1,0:T(8,128)} %copy-done) | copy-start | bytes 6291460
  48.3 1.6 %copy-start.3 = (f32[16,256,128]{2,1,0:T(8,128)S(1)}, f32[16,256,128]{2,1,0:T(8,128)}, u32[]{:S(2)}) copy-start(f32[16,256,128]{2,1,0:T(8,128)} %copy-done.2) | copy-start | bytes 6291460
  49.9 1.1 %copy-start.6 = (bf16[1280,256]{1,0:T(8,128)(2,1)S(1)}, bf16[1280,256]{1,0:T(8,128)(2,1)}, u32[]{:S(2)}) copy-start(bf16[1280,256]{1,0:T(8,128)(2,1)} %copy-done.5) | copy-start | bytes 1966084
  51.0 0.9 %copy-start.9 = (bf16[448,256]{1,0:T(8,128)(2,1)S(1)}, bf16[448,256]{1,0:T(8,128)(2,1)}, u32[]{:S(2)}) copy-start(bf16[448,256]{1,0:T(8,128)(2,1)} %copy-done.8) | copy-start | bytes 688132
  64.9 6.2 %collective-permute-start = (f32[8,2048]{1,0:T(8,128)S(1)}, f32[8,2048]{1,0:T(8,128)S(1)}, u32[]{:S(2)}, u32[]{:S(2)}) collective-permute-start(f32[8,2048]{1,0:T(8,128)S(1)} %get-tuple-element.17), channel_id=1, source_target_pairs={{0,1},{1,2},{2,3},{3,4},{4,5},{5,6},{6,7},{7,8},{8,9},{9,10},{10,1... | collective-permute-start | bytes 196616 | tf_op jit(solution)/shard_map/ppermute | solution.py:356
  68.5 8.3 %collective-permute-start.1 = (f32[8,2048]{1,0:T(8,128)S(1)}, f32[8,2048]{1,0:T(8,128)S(1)}, u32[]{:S(2)}, u32[]{:S(2)}) collective-permute-start(f32[8,2048]{1,0:T(8,128)S(1)} %get-tuple-element.18), channel_id=1, source_target_pairs={{1,0},{2,1},{3,2},{4,3},{5,4},{6,5},{7,6},{8,7},{9,8},{10,9},{11,1... | collective-permute-start | bytes 196616 | tf_op jit(solution)/shard_map/ppermute | solution.py:357

commit v3 on v2

--- a/solution.py
+++ b/solution.py
@@ -16,6 +16,7 @@
 STRIDE = 33
 TAIL = 32
 DIP_REACH = 15
+FILTER_ROWS = 4096
 MERGE = 4
 F32 = jnp.float32
 BF16 = jnp.bfloat16
@@ -115,7 +116,7 @@
         copy.wait()
 
 
-def prepare_kernel(dip, start, weights, heads, tails, turned, place):
+def prepare_kernel(dip, start, weights, filters, moves):
     taps_x = dip.shape[0]
     offsets, samples = start.shape
     bands = []
@@ -128,8 +129,9 @@
         for s in range(2):
             lanes = slice(s * LANES, (s + 1) * LANES)
             if 0 <= d <= taps_x:
-                heads[d * LANES : (d + 1) * LANES, lanes] = pair[s][:LANES]
-            tails[(d + 2) * TAIL : (d + 3) * TAIL, lanes] = pair[s][LANES:]
+                filters[d * LANES : (d + 1) * LANES, lanes] = pair[s][:LANES]
+            tail = (taps_x + 1) * LANES + (d + 2) * TAIL
+            filters[tail : tail + TAIL, lanes] = pair[s][LANES:]
     tile = 8
     sublane = iota((tile, LANES), 0)
 
@@ -142,25 +144,50 @@
                 weights[o, :, pl.ds(at, LANES)].astype(F32), (sublane - first) & (tile - 1), axis=0
             )
             group = ((first - sublane + (tile - 1)) >> 3).astype(F32)
-            rows = slice(o * tile, (o + 1) * tile)
-            turned[j, rows, :] = weight
-            place[j, rows, :] = group
+            row = 2 * o * tile
+            moves[j, row : row + tile, :] = weight
+            moves[j, row + tile : row + 2 * tile, :] = group
         return carry
 
     lax.fori_loop(0, samples // LANES, offset_bands, 0)
 
 
 def stack_kernel(
-    arrived, heads, tails, turned, place, centre, right, left, binned, ends, dipped
+    arrived_hbm,
+    filters_hbm,
+    moves_hbm,
+    centre,
+    right,
+    left,
+    arrived,
+    filters,
+    moves,
+    binned,
+    ends,
+    dipped,
+    sems,
 ):
     slots = arrived.shape[0]
     half = arrived.shape[1] - LANES
-    blocks = turned.shape[0]
-    offsets = turned.shape[1] // 8
+    width = 2 * LANES
+    parts = [(half, half + LANES)] + [(n, n + width) for n in range(0, half, width)]
+    pieces = [
+        (arrived_hbm.at[:, start:stop], arrived.at[:, start:stop]) for start, stop in parts
+    ]
+    pieces += [(filters_hbm.at[: filters.shape[0]], filters), (moves_hbm, moves)]
+    copies = [
+        pltpu.make_async_copy(source, target, sems.at[i])
+        for i, (source, target) in enumerate(pieces)
+    ]
+    for copy in copies:
+        copy.start()
+    blocks = moves.shape[0]
+    offsets = moves.shape[1] // 16
     lines = IL_DEV * offsets
     cells = XL_DEV * lines
     rim = XL_DEV // 2
     out_lines = 2 * XL_DEV
+    copies.pop(0).wait()
     codes = apart(arrived[:, half:])[0]
     rows = codes.T
     code = jnp.where(rows[0:1] > 0.5, rows[1:2] * offsets + rows[2:3], -1.0).astype(jnp.int32)
@@ -171,9 +198,9 @@
     binned[0] = jnp.zeros((XL_DEV, lines, LANES), BF16)
     binned[blocks + 1] = jnp.zeros((XL_DEV, lines, LANES), BF16)
     ends[blocks + 1] = jnp.zeros((2, lines, LANES), BF16)
-    width = 2 * LANES
     lane = iota((lines, LANES), 1)
     for n in range(0, half, width):
+        copies.pop(0).wait()
         parts = apart(arrived[:, n : n + width])
         for h in range(HALVES):
             value = (
@@ -190,7 +217,10 @@
                         end = jnp.where(lane < x * TAIL, end, pltpu.roll(line, x * TAIL, 1))
                     ends[at, g] = end.astype(BF16)
 
+    copies.pop(0).wait()
     group = dipped.shape[0] // STEPS
+
+    tails = (2 * rim + 2) * LANES
 
     def filter_group(step, carry):
         first = step * group
@@ -202,12 +232,12 @@
                 binned[pl.ds(first, group), x].reshape(group * lines, LANES)
                 for x in range(low, high)
             ]
-            rhs = [heads[d * LANES : (d + high - low) * LANES, :]]
+            rhs = [filters[d * LANES : (d + high - low) * LANES, :]]
             for g in range(2):
                 if low < (g + 1) * rim and high > g * rim:
-                    d = g * rim - 2 * pair + 2 * rim + 2
+                    tail = tails + (g * rim - 2 * pair + 2 * rim + 2) * TAIL
                     lhs.append(ends[pl.ds(first + 1, group), g].reshape(group * lines, LANES))
-                    rhs.append(tails[d * TAIL : (d + rim) * TAIL, :])
+                    rhs.append(filters[tail : tail + rim * TAIL, :])
             value = jnp.dot(
                 jnp.concatenate(lhs, axis=1),
                 jnp.concatenate(rhs, axis=0),
@@ -225,6 +255,7 @@
         return carry
 
     lax.fori_loop(0, STEPS, filter_group, 0)
+    copies.pop(0).wait()
 
     span = 2 * out_lines
     root = 1.0 / math.sqrt(offsets)
@@ -236,9 +267,10 @@
         total = jnp.zeros((span, LANES), F32)
         lhs, band = [], []
         for o in range(offsets):
-            weight = turned[j, o * tile : (o + 1) * tile, :]
+            row = 2 * o * tile
+            weight = moves[j, row : row + tile, :]
             weight = jnp.concatenate([weight, weight], axis=0).astype(BF16)
-            group = place[j, o * tile : (o + 1) * tile, :]
+            group = moves[j, row + tile : row + 2 * tile, :]
             group = jnp.concatenate([group, group - 1.0], axis=0).astype(BF16)
             band += [jnp.where(group == float(g), weight, nothing) for g in range(0, 32, 2)]
             rows = pl.ds(o * STRIDE, span)
@@ -295,39 +327,40 @@
     offsets, samples = nmo_start.shape
     taps_x, taps_t = dip_filter.shape
     spread = jnp.pad(dip_filter[:, ::-1].astype(F32), ((0, 0), (2 * LANES - taps_t, 0)))
-    band = jax.ShapeDtypeStruct((samples // LANES, offsets * 8, LANES), F32)
     return pl.pallas_call(
         prepare_kernel,
         out_shape=(
-            jax.ShapeDtypeStruct(((taps_x + 1) * LANES, 2 * LANES), BF16),
-            jax.ShapeDtypeStruct(((taps_x + 5) * TAIL, 2 * LANES), BF16),
-            band,
-            band,
+            jax.ShapeDtypeStruct((FILTER_ROWS, 2 * LANES), BF16),
+            jax.ShapeDtypeStruct((samples // LANES, offsets * 16, LANES), F32),
         ),
         in_specs=whole(3),
-        out_specs=tuple(whole(4)),
+        out_specs=tuple(whole(2)),
         compiler_params=pltpu.CompilerParams(vmem_limit_bytes=20 * 2**20),
     )(spread, nmo_start, nmo_weights)
 
 
-def stack_call(arrived, heads, tails, turned, place):
-    blocks = turned.shape[0]
-    offsets = turned.shape[1] // 8
+def stack_call(arrived, filters, moves):
+    blocks = moves.shape[0]
+    offsets = moves.shape[1] // 16
     samples = blocks * LANES
     lines = IL_DEV * offsets
     edge = jax.ShapeDtypeStruct((IL_DEV * XL_DEV // 2, samples), F32)
     return pl.pallas_call(
         stack_kernel,
         out_shape=(jax.ShapeDtypeStruct((IL_DEV, XL_DEV, samples), F32), edge, edge),
-        in_specs=whole(5),
+        in_specs=[pl.BlockSpec(memory_space=pl.ANY)] * 3,
         out_specs=tuple(whole(3)),
         scratch_shapes=[
+            pltpu.VMEM(arrived.shape, BF16),
+            pltpu.VMEM(((XL_DEV + 2) * LANES + (XL_DEV + 6) * TAIL, 2 * LANES), BF16),
+            pltpu.VMEM(moves.shape, F32),
             pltpu.VMEM((blocks + 2, XL_DEV, lines, LANES), BF16),
             pltpu.VMEM((blocks + 3, 2, lines, LANES), BF16),
             pltpu.VMEM((blocks + 2, offsets * STRIDE, LANES), F32),
+            pltpu.SemaphoreType.DMA((3 + samples // HALVES // (2 * LANES),)),
         ],
-        compiler_params=pltpu.CompilerParams(vmem_limit_bytes=30 * 2**20),
-    )(arrived, heads, tails, turned, place)
+        compiler_params=pltpu.CompilerParams(vmem_limit_bytes=50 * 2**20),
+    )(arrived, filters, moves)
 
 
 def per_device(

time: 77.9 us -> 74.7 us (0.959)
  local copies, waits for them, and re-layouts: 10.5 us -> 2.1 us
  waiting for transfers between devices: 31.3 us -> 34.2 us
  Pallas kernels: 18.5 us -> 20.5 us
    unnamed x22 -> x8, local copies, waits for them, and re-layouts: 10.4 us -> 1.96 us
    all_to_all x1, waiting for transfers between devices: 25.2 us -> 28.2 us  [per_device(): lax.all_to_all(outgoing.reshape(owners, rows // owners, width), ('shot',...]
    pallas_call x1, Pallas kernels: 13 us -> 14.9 us  [stack_call(): pl.pallas_call(stack_kernel, out_shape=(jax.ShapeDtypeStruct((IL_DEV, XL_...]
where the time goes in v3:
time: 74.7 us; the launch traced here: 74.4 us
  waiting for transfers between devices  34.2 us (46%)
  Pallas kernels  20.5 us (27%)
  starting transfers between devices  16.7 us (22%)
  local copies, waits for them, and re-layouts  2.1 us (3%)
  other arithmetic  0.77 us (1%)
    all_to_all x1, waiting for transfers between devices, per_device(): lax.all_to_all(outgoing.reshape(owners, rows // owners, width), ('shot',...  28.2 us
    pallas_call x1, Pallas kernels, stack_call(): pl.pallas_call(stack_kernel, out_shape=(jax.ShapeDtypeStruct((IL_DEV, XL_...  14.9 us
    all_to_all x1, starting transfers between devices, per_device(): lax.all_to_all(outgoing.reshape(owners, rows // owners, width), ('shot',...  10.9 us
    ppermute x1, waiting for transfers between devices, per_device(): from_right = lax.ppermute(left, 'bin', [(i + 1, i) for i in ends])  5.67 us
    pallas_call x1, Pallas kernels, send_call(): pl.pallas_call(send_kernel, out_shape=jax.ShapeDtypeStruct((owners * per_...  4.35 us
    ppermute x1, starting transfers between devices, per_device(): from_left = lax.ppermute(right, 'bin', [(i, i + 1) for i in ends])  3.65 us
    ppermute x1, starting transfers between devices, per_device(): from_right = lax.ppermute(left, 'bin', [(i + 1, i) for i in ends])  2.19 us
    unnamed x8, local copies, waits for them, and re-layouts  1.96 us
  transfers between devices with their start and end apart: 3, of which 3 were waited for; matrix products, arithmetic and copies ran while one was open for 0% of the time, Pallas kernels for 2%

profile of v3, /device:TPU:6, one launch (start us, length us, event | category | flops | bytes accessed | tf_op | source)
XLA Modules:
  0.0 74.4 jit_solution(16459205553157864109)
XLA Ops:
  0.0 4.3 %shard_map.91 = bf16[1024,1152]{1,0:T(8,128)(2,1)} custom-call(bf16[256,2048]{1,0:T(8,128)(2,1)} %traces_hbm.1, bf16[1,128]{1,0:T(2,128)(2,1)} %shot_filter.1, f32[1,256]{1,0:T(1,128)} %bitcast.7, s32[1,256]{1,0:T(1,128)} %bitcast.8, s32[1,256]{1,0:T(1,128)} %bitcast.9, s32[1,256]{1,0:T(1,128)} %bitcast.10), custom_call_target="tpu_custom_call" | custom-call | tf_op jit(solution)/shard_map/pallas_call | solution.py:305
  4.4 0.0 copy-start.3
  4.4 0.0 copy-start.1
  4.4 0.0 copy-start.2
  4.4 10.9 %all-to-all-start = ((bf16[128,8,1152]{2,1,0:T(8,128)(2,1)}), bf16[128,8,1152]{2,1,0:T(8,128)(2,1)}, u32[]{:S(2)}, u32[]{:S(2)}) async-start(bf16[128,8,1152]{2,1,0:T(8,128)(2,1)} %bitcast.6), calls=%async_computation | async-start | bytes 4718592 | tf_op jit(solution)/shard_map/all_to_all | solution.py:382
  15.3 0.0 copy-done.3
  15.3 0.1 rev.3
  15.4 0.1 pad_convert_fusion.dip
  15.5 0.0 copy-done.1
  15.5 0.0 copy-done.2
  15.5 1.2 %shard_map.92 = (bf16[4096,256]{1,0:T(8,128)(2,1)S(1)}, f32[16,512,128]{2,1,0:T(8,128)S(1)}) custom-call(f32[9,256]{1,0:T(8,128)S(1)} %pad_convert_fusion.dip, s32[32,2048]{1,0:T(8,128)S(1)} %copy-done.2, bf16[32,8,2048]{2,1,0:T(8,128)(2,1)S(1)} %copy-done.1), custom_call_target="tpu_custom_call" | custom-call | tf_op jit(solution)/shard_map/pallas_call | solution.py:330
  16.7 0.0 copy-start
  16.7 1.9 %copy-done = f32[16,512,128]{2,1,0:T(8,128)} copy-done((f32[16,512,128]{2,1,0:T(8,128)}, f32[16,512,128]{2,1,0:T(8,128)S(1)}, u32[]{:S(2)}) %copy-start) | copy-done | bytes 4194328
  18.6 28.2 %all-to-all-done = bf16[128,8,1152]{2,1,0:T(8,128)(2,1)} async-done(((bf16[128,8,1152]{2,1,0:T(8,128)(2,1)}), bf16[128,8,1152]{2,1,0:T(8,128)(2,1)}, u32[]{:S(2)}, u32[]{:S(2)}) %all-to-all-start) | async-done | bytes 2359328 | tf_op jit(solution)/shard_map/all_to_all | solution.py:382
  46.8 14.9 %shard_map.93 = (f32[2,8,2048]{2,1,0:T(8,128)S(1)}, f32[8,2048]{1,0:T(8,128)S(1)}, f32[8,2048]{1,0:T(8,128)S(1)}) custom-call(bf16[1024,1152]{1,0:T(8,128)(2,1)} %bitcast.5.arrived_hbm, bf16[4096,256]{1,0:T(8,128)(2,1)S(1)} %get-tuple-element.10.filters_hbm, f32[16,512,128]{2,1,0:T(8,128)} %copy-done), custom_call_target="tpu_custom_call" | custom-call | tf_op jit(solution)/shard_map/pallas_call | solution.py:348
  61.8 3.7 %collective-permute-start = (f32[8,2048]{1,0:T(8,128)S(1)}, f32[8,2048]{1,0:T(8,128)S(1)}, u32[]{:S(2)}, u32[]{:S(2)}) collective-permute-start(f32[8,2048]{1,0:T(8,128)S(1)} %get-tuple-element.13), channel_id=1, source_target_pairs={{0,1},{1,2},{2,3},{3,4},{4,5},{5,6},{6,7},{7,8},{8,9},{9,10},{10,1... | collective-permute-start | bytes 196616 | tf_op jit(solution)/shard_map/ppermute | solution.py:389
  65.4 2.2 %collective-permute-start.1 = (f32[8,2048]{1,0:T(8,128)S(1)}, f32[8,2048]{1,0:T(8,128)S(1)}, u32[]{:S(2)}, u32[]{:S(2)}) collective-permute-start(f32[8,2048]{1,0:T(8,128)S(1)} %get-tuple-element.14), channel_id=1, source_target_pairs={{1,0},{2,1},{3,2},{4,3},{5,4},{6,5},{7,6},{8,7},{9,8},{10,9},{11,1... | collective-permute-start | bytes 196616 | tf_op jit(solution)/shard_map/ppermute | solution.py:390
  67.6 0.4 collective-permute-done
  68.0 5.7 %collective-permute-done.1 = f32[8,2048]{1,0:T(8,128)S(1)} collective-permute-done((f32[8,2048]{1,0:T(8,128)S(1)}, f32[8,2048]{1,0:T(8,128)S(1)}, u32[]{:S(2)}, u32[]{:S(2)}) %collective-permute-start.1) | collective-permute-done | bytes 65568 | tf_op jit(solution)/shard_map/ppermute | solution.py:390
  73.7 0.7 maximum_add_fusion
  (2 shorter events, 0.0 us)
Async XLA Ops:
  4.4 10.9 %copy-start.3 = (bf16[9,31]{1,0:T(8,128)(2,1)S(1)}, bf16[9,31]{1,0:T(8,128)(2,1)}, u32[]{:S(2)}) copy-start(bf16[9,31]{1,0:T(8,128)(2,1)} %param.15) | copy-start | bytes 1678
  4.4 11.1 %copy-start.1 = (bf16[32,8,2048]{2,1,0:T(8,128)(2,1)S(1)}, bf16[32,8,2048]{2,1,0:T(8,128)(2,1)}, u32[]{:S(2)}) copy-start(bf16[32,8,2048]{2,1,0:T(8,128)(2,1)} %weights.1) | copy-start | bytes 3145732
  4.4 11.1 %copy-start.2 = (s32[32,2048]{1,0:T(8,128)S(1)}, s32[32,2048]{1,0:T(8,128)}, u32[]{:S(2)}) copy-start(s32[32,2048]{1,0:T(8,128)} %start.1) | copy-start | bytes 786436
  4.4 42.5 %all-to-all-start = ((bf16[128,8,1152]{2,1,0:T(8,128)(2,1)}), bf16[128,8,1152]{2,1,0:T(8,128)(2,1)}, u32[]{:S(2)}, u32[]{:S(2)}) async-start(bf16[128,8,1152]{2,1,0:T(8,128)(2,1)} %bitcast.6), calls=%async_computation | async-start | bytes 4718592 | tf_op jit(solution)/shard_map/all_to_all | solution.py:382
  16.7 1.9 %copy-start = (f32[16,512,128]{2,1,0:T(8,128)}, f32[16,512,128]{2,1,0:T(8,128)S(1)}, u32[]{:S(2)}) copy-start(f32[16,512,128]{2,1,0:T(8,128)S(1)} %get-tuple-element.11.moves_hbm) | copy-start | bytes 12582916
  61.8 6.2 %collective-permute-start = (f32[8,2048]{1,0:T(8,128)S(1)}, f32[8,2048]{1,0:T(8,128)S(1)}, u32[]{:S(2)}, u32[]{:S(2)}) collective-permute-start(f32[8,2048]{1,0:T(8,128)S(1)} %get-tuple-element.13), channel_id=1, source_target_pairs={{0,1},{1,2},{2,3},{3,4},{4,5},{5,6},{6,7},{7,8},{8,9},{9,10},{10,1... | collective-permute-start | bytes 196616 | tf_op jit(solution)/shard_map/ppermute | solution.py:389
  65.4 8.3 %collective-permute-start.1 = (f32[8,2048]{1,0:T(8,128)S(1)}, f32[8,2048]{1,0:T(8,128)S(1)}, u32[]{:S(2)}, u32[]{:S(2)}) collective-permute-start(f32[8,2048]{1,0:T(8,128)S(1)} %get-tuple-element.14), channel_id=1, source_target_pairs={{1,0},{2,1},{3,2},{4,3},{5,4},{6,5},{7,6},{8,7},{9,8},{10,9},{11,1... | collective-permute-start | bytes 196616 | tf_op jit(solution)/shard_map/ppermute | solution.py:390

commit v4 on v3

--- a/solution.py
+++ b/solution.py
@@ -16,7 +16,7 @@
 STRIDE = 33
 TAIL = 32
 DIP_REACH = 15
-FILTER_ROWS = 4096
+FILTER_ROWS = 8192
 MERGE = 4
 F32 = jnp.float32
 BF16 = jnp.bfloat16
@@ -46,11 +46,40 @@
 
 
 def send_kernel(
-    traces_hbm, shot_filter, gain, owner, slot, offset, out_hbm, traces, out, filtered, sems
+    traces_hbm,
+    shot_filter_hbm,
+    gain_hbm,
+    owner_hbm,
+    slot_hbm,
+    offset_hbm,
+    out_hbm,
+    shot_filter,
+    gain,
+    owner,
+    slot,
+    offset,
+    traces,
+    out,
+    filtered,
+    sems,
+    small_sems,
 ):
     rows, samples = traces.shape
     blocks = samples // LANES
     half = samples // HALVES
+    pieces = [
+        (owner_hbm, owner),
+        (slot_hbm, slot),
+        (offset_hbm, offset),
+        (gain_hbm, gain),
+        (shot_filter_hbm, shot_filter),
+    ]
+    small = [
+        pltpu.make_async_copy(source, target, small_sems.at[i])
+        for i, (source, target) in enumerate(pieces)
+    ]
+    for copy in small:
+        copy.start()
     fetch = pltpu.make_async_copy(traces_hbm, traces, sems.at[0])
     fetch.start()
     copies = []
@@ -63,6 +92,8 @@
         copy.start()
         copies.append(copy)
 
+    for copy in small:
+        copy.wait()
     slots = slot[...]
     hi = (slots % XL_DEV) * IL_DEV + slots // XL_DEV
     lo = offset[...]
@@ -145,21 +176,19 @@
             )
             group = ((first - sublane + (tile - 1)) >> 3).astype(F32)
             row = 2 * o * tile
-            moves[j, row : row + tile, :] = weight
-            moves[j, row + tile : row + 2 * tile, :] = group
+            moves[j, row : row + 2 * tile, :] = jnp.concatenate([weight, group], axis=0).astype(BF16)
         return carry
 
     lax.fori_loop(0, samples // LANES, offset_bands, 0)
 
 
 def stack_kernel(
-    arrived_hbm,
+    arrived,
     filters_hbm,
     moves_hbm,
     centre,
     right,
     left,
-    arrived,
     filters,
     moves,
     binned,
@@ -170,11 +199,7 @@
     slots = arrived.shape[0]
     half = arrived.shape[1] - LANES
     width = 2 * LANES
-    parts = [(half, half + LANES)] + [(n, n + width) for n in range(0, half, width)]
-    pieces = [
-        (arrived_hbm.at[:, start:stop], arrived.at[:, start:stop]) for start, stop in parts
-    ]
-    pieces += [(filters_hbm.at[: filters.shape[0]], filters), (moves_hbm, moves)]
+    pieces = [(filters_hbm.at[: filters.shape[0]], filters), (moves_hbm, moves)]
     copies = [
         pltpu.make_async_copy(source, target, sems.at[i])
         for i, (source, target) in enumerate(pieces)
@@ -187,7 +212,6 @@
     cells = XL_DEV * lines
     rim = XL_DEV // 2
     out_lines = 2 * XL_DEV
-    copies.pop(0).wait()
     codes = apart(arrived[:, half:])[0]
     rows = codes.T
     code = jnp.where(rows[0:1] > 0.5, rows[1:2] * offsets + rows[2:3], -1.0).astype(jnp.int32)
@@ -200,7 +224,6 @@
     ends[blocks + 1] = jnp.zeros((2, lines, LANES), BF16)
     lane = iota((lines, LANES), 1)
     for n in range(0, half, width):
-        copies.pop(0).wait()
         parts = apart(arrived[:, n : n + width])
         for h in range(HALVES):
             value = (
@@ -268,9 +291,9 @@
         lhs, band = [], []
         for o in range(offsets):
             row = 2 * o * tile
-            weight = moves[j, row : row + tile, :]
+            weight = moves[j, row : row + tile, :].astype(F32)
             weight = jnp.concatenate([weight, weight], axis=0).astype(BF16)
-            group = moves[j, row + tile : row + 2 * tile, :]
+            group = moves[j, row + tile : row + 2 * tile, :].astype(F32)
             group = jnp.concatenate([group, group - 1.0], axis=0).astype(BF16)
             band += [jnp.where(group == float(g), weight, nothing) for g in range(0, 32, 2)]
             rows = pl.ds(o * STRIDE, span)
@@ -287,8 +310,8 @@
             base = i * out_lines
             edge = pl.ds(i * rim, rim)
             centre[i, :, pl.ds(at, LANES)] = total[base : base + XL_DEV, :]
-            right[edge, pl.ds(at, LANES)] = total[base + XL_DEV : base + XL_DEV + rim, :]
-            left[edge, pl.ds(at, LANES)] = total[base + XL_DEV + rim : base + out_lines, :]
+            right[edge, pl.ds(at, LANES)] = total[base + XL_DEV : base + XL_DEV + rim, :].astype(BF16)
+            left[edge, pl.ds(at, LANES)] = total[base + XL_DEV + rim : base + out_lines, :].astype(BF16)
         return carry
 
     lax.fori_loop(0, blocks, move_out, 0)
@@ -305,13 +328,19 @@
     return pl.pallas_call(
         send_kernel,
         out_shape=jax.ShapeDtypeStruct((owners * per_owner, width), BF16),
-        in_specs=[pl.BlockSpec(memory_space=pl.ANY)] + whole(5),
+        in_specs=[pl.BlockSpec(memory_space=pl.ANY)] * 6,
         out_specs=pl.BlockSpec(memory_space=pl.ANY),
         scratch_shapes=[
+            pltpu.VMEM(shot_filter.shape, BF16),
+            pltpu.VMEM((1, rows), F32),
+            pltpu.VMEM((1, rows), jnp.int32),
+            pltpu.VMEM((1, rows), jnp.int32),
+            pltpu.VMEM((1, rows), jnp.int32),
             pltpu.VMEM((rows, samples), BF16),
             pltpu.VMEM((owners * per_owner, width), BF16),
             pltpu.VMEM((HALVES * rows, samples // HALVES), BF16),
             pltpu.SemaphoreType.DMA((2 + samples // HALVES // (2 * LANES),)),
+            pltpu.SemaphoreType.DMA((5,)),
         ],
     )(
         traces,
@@ -331,7 +360,7 @@
         prepare_kernel,
         out_shape=(
             jax.ShapeDtypeStruct((FILTER_ROWS, 2 * LANES), BF16),
-            jax.ShapeDtypeStruct((samples // LANES, offsets * 16, LANES), F32),
+            jax.ShapeDtypeStruct((samples // LANES, offsets * 16, LANES), BF16),
         ),
         in_specs=whole(3),
         out_specs=tuple(whole(2)),
@@ -344,22 +373,21 @@
     offsets = moves.shape[1] // 16
     samples = blocks * LANES
     lines = IL_DEV * offsets
-    edge = jax.ShapeDtypeStruct((IL_DEV * XL_DEV // 2, samples), F32)
+    edge = jax.ShapeDtypeStruct((IL_DEV * XL_DEV // 2, samples), BF16)
     return pl.pallas_call(
         stack_kernel,
         out_shape=(jax.ShapeDtypeStruct((IL_DEV, XL_DEV, samples), F32), edge, edge),
-        in_specs=[pl.BlockSpec(memory_space=pl.ANY)] * 3,
+        in_specs=whole(1) + [pl.BlockSpec(memory_space=pl.ANY)] * 2,
         out_specs=tuple(whole(3)),
         scratch_shapes=[
-            pltpu.VMEM(arrived.shape, BF16),
             pltpu.VMEM(((XL_DEV + 2) * LANES + (XL_DEV + 6) * TAIL, 2 * LANES), BF16),
-            pltpu.VMEM(moves.shape, F32),
+            pltpu.VMEM(moves.shape, BF16),
             pltpu.VMEM((blocks + 2, XL_DEV, lines, LANES), BF16),
             pltpu.VMEM((blocks + 3, 2, lines, LANES), BF16),
             pltpu.VMEM((blocks + 2, offsets * STRIDE, LANES), F32),
-            pltpu.SemaphoreType.DMA((3 + samples // HALVES // (2 * LANES),)),
+            pltpu.SemaphoreType.DMA((2,)),
         ],
-        compiler_params=pltpu.CompilerParams(vmem_limit_bytes=50 * 2**20),
+        compiler_params=pltpu.CompilerParams(vmem_limit_bytes=49 * 2**20),
     )(arrived, filters, moves)
 
 
@@ -391,7 +419,7 @@
     shape = (IL_DEV, XL_DEV // 2, centre.shape[2])
     return centre + jnp.concatenate(
         [from_left.reshape(shape), from_right.reshape(shape)], axis=1
-    )
+    ).astype(F32)
 
 
 def solution(mesh):

time: 74.7 us -> 73.4 us (0.983)
  local copies, waits for them, and re-layouts: 2.1 us -> 6.02 us
  waiting for transfers between devices: 34.2 us -> 31.7 us
  Pallas kernels: 20.5 us -> 18.2 us
    unnamed x8 -> x12, local copies, waits for them, and re-layouts: 1.96 us -> 5.89 us
    all_to_all x1, waiting for transfers between devices: 28.2 us -> 26.1 us  [per_device(): lax.all_to_all(outgoing.reshape(owners, rows // owners, width), ('shot',...]
    pallas_call x1, Pallas kernels: 14.9 us -> 13.2 us  [stack_call(): pl.pallas_call(stack_kernel, out_shape=(jax.ShapeDtypeStruct((IL_DEV, XL_...]
  transfers between devices with their start and end apart: 3 -> 3, of which waited for: 3 -> 2; matrix products, arithmetic and copies ran while one was open for 0% -> 0% of each run, Pallas kernels for 2% -> 2%
where the time goes in v4:
time: 73.4 us; the launch traced here: 73.2 us
  waiting for transfers between devices  31.7 us (43%)
  Pallas kernels  18.2 us (25%)
  starting transfers between devices  16.3 us (22%)
  local copies, waits for them, and re-layouts  6.02 us (8%)
  other arithmetic  0.77 us (1%)
    all_to_all x1, waiting for transfers between devices, per_device(): lax.all_to_all(outgoing.reshape(owners, rows // owners, width), ('shot',...  26.1 us
    pallas_call x1, Pallas kernels, stack_call(): pl.pallas_call(stack_kernel, out_shape=(jax.ShapeDtypeStruct((IL_DEV, XL_...  13.2 us
    all_to_all x1, starting transfers between devices, per_device(): lax.all_to_all(outgoing.reshape(owners, rows // owners, width), ('shot',...  10.5 us
    unnamed x12, local copies, waits for them, and re-layouts  5.89 us
    ppermute x1, waiting for transfers between devices, per_device(): from_right = lax.ppermute(left, 'bin', [(i + 1, i) for i in ends])  5.68 us
    pallas_call x1, Pallas kernels, send_call(): pl.pallas_call(send_kernel, out_shape=jax.ShapeDtypeStruct((owners * per_...  3.72 us
    ppermute x1, starting transfers between devices, per_device(): from_left = lax.ppermute(right, 'bin', [(i, i + 1) for i in ends])  3.65 us
    ppermute x1, starting transfers between devices, per_device(): from_right = lax.ppermute(left, 'bin', [(i + 1, i) for i in ends])  2.19 us
  transfers between devices with their start and end apart: 3, of which 2 were waited for; matrix products, arithmetic and copies ran while one was open for 0% of the time, Pallas kernels for 2%

profile of v4, /device:TPU:6, one launch (start us, length us, event | category | flops | bytes accessed | tf_op | source)
XLA Modules:
  0.0 73.2 jit_solution(4170527828538833009)
XLA Ops:
  0.0 3.7 %shard_map.91 = bf16[1024,1152]{1,0:T(8,128)(2,1)} custom-call(bf16[256,2048]{1,0:T(8,128)(2,1)} %traces_hbm.1, bf16[1,128]{1,0:T(2,128)(2,1)} %shot_filter_hbm.1, f32[1,256]{1,0:T(1,128)} %bitcast.8, s32[1,256]{1,0:T(1,128)} %bitcast.9, s32[1,256]{1,0:T(1,128)} %bitcast.10, s32[1,256]{1,0:T(1,128)} %bitcast.11), custom_call_target="tpu_custom_call" | custom-call | tf_op jit(solution)/shard_map/pallas_call | solution.py:328
  3.7 0.0 copy-start.5
  3.7 0.0 copy-start.3
  3.7 10.5 %all-to-all-start = ((bf16[128,8,1152]{2,1,0:T(8,128)(2,1)}), bf16[128,8,1152]{2,1,0:T(8,128)(2,1)S(1)}, u32[]{:S(2)}, u32[]{:S(2)}) async-start(bf16[128,8,1152]{2,1,0:T(8,128)(2,1)} %bitcast.7), calls=%async_computation | async-start | bytes 4718592 | tf_op jit(solution)/shard_map/all_to_all | solution.py:410
  14.2 0.0 copy-done.5
  14.2 0.1 rev.3
  14.3 0.1 pad_convert_fusion.dip
  14.4 0.0 copy-done.3
  14.4 0.0 copy-start.4
  14.4 0.9 %copy-done.4 = s32[32,2048]{1,0:T(8,128)S(1)} copy-done((s32[32,2048]{1,0:T(8,128)S(1)}, s32[32,2048]{1,0:T(8,128)}, u32[]{:S(2)}) %copy-start.4) | copy-done | bytes 262168
  15.4 1.3 %shard_map.92 = (bf16[8192,256]{1,0:T(8,128)(2,1)S(1)}, bf16[16,512,128]{2,1,0:T(8,128)(2,1)S(1)}) custom-call(f32[9,256]{1,0:T(8,128)S(1)} %pad_convert_fusion.dip, s32[32,2048]{1,0:T(8,128)S(1)} %copy-done.4, bf16[32,8,2048]{2,1,0:T(8,128)(2,1)S(1)} %copy-done.3), custom_call_target="tpu_custom_call" | custom-call | tf_op jit(solution)/shard_map/pallas_call | solution.py:359
  16.7 0.0 copy-start
  16.7 1.9 %copy-done = bf16[8192,256]{1,0:T(8,128)(2,1)} copy-done((bf16[8192,256]{1,0:T(8,128)(2,1)}, bf16[8192,256]{1,0:T(8,128)(2,1)S(1)}, u32[]{:S(2)}) %copy-start) | copy-done | bytes 4194328
  18.6 0.0 copy-start.1
  18.6 1.4 %copy-done.1 = bf16[16,512,128]{2,1,0:T(8,128)(2,1)} copy-done((bf16[16,512,128]{2,1,0:T(8,128)(2,1)}, bf16[16,512,128]{2,1,0:T(8,128)(2,1)S(1)}, u32[]{:S(2)}) %copy-start.1) | copy-done | bytes 2097176
  20.0 26.1 %all-to-all-done = bf16[128,8,1152]{2,1,0:T(8,128)(2,1)S(1)} async-done(((bf16[128,8,1152]{2,1,0:T(8,128)(2,1)}), bf16[128,8,1152]{2,1,0:T(8,128)(2,1)S(1)}, u32[]{:S(2)}, u32[]{:S(2)}) %all-to-all-start) | async-done | bytes 2359328 | tf_op jit(solution)/shard_map/all_to_all | solution.py:410
  46.1 0.0 copy-start.2
  46.1 1.6 %copy-done.2 = bf16[16,512,128]{2,1,0:T(8,128)(2,1)S(1)} copy-done((bf16[16,512,128]{2,1,0:T(8,128)(2,1)S(1)}, bf16[16,512,128]{2,1,0:T(8,128)(2,1)}, u32[]{:S(2)}) %copy-start.2) | copy-done | bytes 2097176
  47.7 13.2 %shard_map.93 = (f32[2,8,2048]{2,1,0:T(8,128)S(1)}, bf16[8,2048]{1,0:T(8,128)(2,1)S(1)}, bf16[8,2048]{1,0:T(8,128)(2,1)S(1)}) custom-call(bf16[1024,1152]{1,0:T(8,128)(2,1)S(1)} %bitcast.6, bf16[8192,256]{1,0:T(8,128)(2,1)} %copy-done, bf16[16,512,128]{2,1,0:T(8,128)(2,1)S(1)} %copy-done.2), custom_call_target="tpu_custom_call" | custom-call | tf_op jit(solution)/shard_map/pallas_call | solution.py:377
  60.9 3.7 %collective-permute-start = (bf16[8,2048]{1,0:T(8,128)(2,1)S(1)}, bf16[8,2048]{1,0:T(8,128)(2,1)S(1)}, u32[]{:S(2)}, u32[]{:S(2)}) collective-permute-start(bf16[8,2048]{1,0:T(8,128)(2,1)S(1)} %get-tuple-element.13), channel_id=1, source_target_pairs={{0,1},{1,2},{2,3},{3,4},{4,5},{5,6},{6,7},{7,8},{8,9},{9,10},{10,1... | collective-permute-start | bytes 98312 | tf_op jit(solution)/shard_map/ppermute | solution.py:417
  64.5 2.2 %collective-permute-start.1 = (bf16[8,2048]{1,0:T(8,128)(2,1)S(1)}, bf16[8,2048]{1,0:T(8,128)(2,1)S(1)}, u32[]{:S(2)}, u32[]{:S(2)}) collective-permute-start(bf16[8,2048]{1,0:T(8,128)(2,1)S(1)} %get-tuple-element.14), channel_id=1, source_target_pairs={{1,0},{2,1},{3,2},{4,3},{5,4},{6,5},{7,6},{8,7},{9,8},{10,9},{11,1... | collective-permute-start | bytes 98312 | tf_op jit(solution)/shard_map/ppermute | solution.py:418
  66.7 0.0 collective-permute-done
  66.8 5.7 %collective-permute-done.1 = bf16[8,2048]{1,0:T(8,128)(2,1)S(1)} collective-permute-done((bf16[8,2048]{1,0:T(8,128)(2,1)S(1)}, bf16[8,2048]{1,0:T(8,128)(2,1)S(1)}, u32[]{:S(2)}, u32[]{:S(2)}) %collective-permute-start.1) | collective-permute-done | bytes 32800 | tf_op jit(solution)/shard_map/ppermute | solution.py:418
  72.5 0.7 convert_add_fusion
  (2 shorter events, 0.0 us)
Async XLA Ops:
  3.7 10.5 %copy-start.5 = (bf16[9,31]{1,0:T(8,128)(2,1)S(1)}, bf16[9,31]{1,0:T(8,128)(2,1)}, u32[]{:S(2)}) copy-start(bf16[9,31]{1,0:T(8,128)(2,1)} %param.15) | copy-start | bytes 1678
  3.7 10.7 %copy-start.3 = (bf16[32,8,2048]{2,1,0:T(8,128)(2,1)S(1)}, bf16[32,8,2048]{2,1,0:T(8,128)(2,1)}, u32[]{:S(2)}) copy-start(bf16[32,8,2048]{2,1,0:T(8,128)(2,1)} %weights.1) | copy-start | bytes 3145732
  3.7 42.3 %all-to-all-start = ((bf16[128,8,1152]{2,1,0:T(8,128)(2,1)}), bf16[128,8,1152]{2,1,0:T(8,128)(2,1)S(1)}, u32[]{:S(2)}, u32[]{:S(2)}) async-start(bf16[128,8,1152]{2,1,0:T(8,128)(2,1)} %bitcast.7), calls=%async_computation | async-start | bytes 4718592 | tf_op jit(solution)/shard_map/all_to_all | solution.py:410
  14.4 1.0 %copy-start.4 = (s32[32,2048]{1,0:T(8,128)S(1)}, s32[32,2048]{1,0:T(8,128)}, u32[]{:S(2)}) copy-start(s32[32,2048]{1,0:T(8,128)} %start.1) | copy-start | bytes 786436
  16.7 2.0 %copy-start = (bf16[8192,256]{1,0:T(8,128)(2,1)}, bf16[8192,256]{1,0:T(8,128)(2,1)S(1)}, u32[]{:S(2)}) copy-start(bf16[8192,256]{1,0:T(8,128)(2,1)S(1)} %get-tuple-element.10.filters_hbm) | copy-start | bytes 12582916
  18.6 1.4 %copy-start.1 = (bf16[16,512,128]{2,1,0:T(8,128)(2,1)}, bf16[16,512,128]{2,1,0:T(8,128)(2,1)S(1)}, u32[]{:S(2)}) copy-start(bf16[16,512,128]{2,1,0:T(8,128)(2,1)S(1)} %get-tuple-element.11.moves_hbm) | copy-start | bytes 6291460
  46.1 1.6 %copy-start.2 = (bf16[16,512,128]{2,1,0:T(8,128)(2,1)S(1)}, bf16[16,512,128]{2,1,0:T(8,128)(2,1)}, u32[]{:S(2)}) copy-start(bf16[16,512,128]{2,1,0:T(8,128)(2,1)} %copy-done.1) | copy-start | bytes 6291460
  60.9 5.9 %collective-permute-start = (bf16[8,2048]{1,0:T(8,128)(2,1)S(1)}, bf16[8,2048]{1,0:T(8,128)(2,1)S(1)}, u32[]{:S(2)}, u32[]{:S(2)}) collective-permute-start(bf16[8,2048]{1,0:T(8,128)(2,1)S(1)} %get-tuple-element.13), channel_id=1, source_target_pairs={{0,1},{1,2},{2,3},{3,4},{4,5},{5,6},{6,7},{7,8},{8,9},{9,10},{10,1... | collective-permute-start | bytes 98312 | tf_op jit(solution)/shard_map/ppermute | solution.py:417
  64.5 7.9 %collective-permute-start.1 = (bf16[8,2048]{1,0:T(8,128)(2,1)S(1)}, bf16[8,2048]{1,0:T(8,128)(2,1)S(1)}, u32[]{:S(2)}, u32[]{:S(2)}) collective-permute-start(bf16[8,2048]{1,0:T(8,128)(2,1)S(1)} %get-tuple-element.14), channel_id=1, source_target_pairs={{1,0},{2,1},{3,2},{4,3},{5,4},{6,5},{7,6},{8,7},{9,8},{10,9},{11,1... | collective-permute-start | bytes 98312 | tf_op jit(solution)/shard_map/ppermute | solution.py:418
